TPU v7x, 256 devices: a whole 4x4x8 slice. The times are simulated.
256 devices in a mesh: band: 64 (over x, y_lo, z), comp: 2 (over y_hi), tile: 2 (over core).
Axes of the slice: x: 4, y: 4 (y_hi: 2, y_lo: 2; y = y_hi * 2 + y_lo), z: 8, core: 2. Of those that a mesh axis runs over, the one named last changes fastest.
Arguments:
- atmosphere: bfloat16 [192, 384, 768], P('band', None, ('comp', 'tile')), may hold values from -6 to 6
- spec_weight: float32 [2, 2, 2, 768, 96], P(None, None, None, ('comp', 'tile')), may hold values from -0.625 to 0.625
- spec_bias: float32 [2, 2, 2, 768], P(None, None, None, ('comp', 'tile')), may hold values from -4 to 4
- norm_gain: float32 [2, 2, 768], replicated, may hold values from 0.25 to 1.75
- norm_shift: float32 [2, 2, 768], replicated, may hold values from -3 to 3
- fc_in: bfloat16 [2, 768, 3072], P(None, None, ('comp', 'tile')), may hold values from -0.21875 to 0.21875
- fc_out: bfloat16 [2, 3072, 768], P(None, ('comp', 'tile')), may hold values from -0.109375 to 0.109375
- flux_head: bfloat16 [768, 8], P(('comp', 'tile')), may hold values from -0.21875 to 0.21875
- flux_embed: float32 [8, 256], replicated, may hold values from -2 to 2
- ocean_state: bfloat16 [384, 768, 256], P('band', ('comp', 'tile')), may hold values from -6 to 6
- sea_mask: int32 [384, 768], P('band', ('comp', 'tile')), may hold values 0 or 1
- depth_kernel: float32 [7, 7, 256], replicated, may hold values from -0.875 to 0.875
- ocean_gain: float32 [256], replicated, may hold values from 0.25 to 1.75
- ocean_shift: float32 [256], replicated, may hold values from -3 to 3
- ocean_in: bfloat16 [256, 1024], replicated, may hold values from -0.375 to 0.375
- ocean_out: bfloat16 [1024, 256], replicated, may hold values from -0.1875 to 0.1875
- layer_scale: float32 [256], replicated, may hold values from 0.3 to 1
- field_head: float32 [256, 4], replicated, may hold values from -0.375 to 0.375
- patch_embed: float32 [16, 768], P(None, ('comp', 'tile')), may hold values from -1.5 to 1.5
Outputs:
- atmosphere_next: bfloat16 [192, 384, 768], P('band', None, ('comp', 'tile'))
- ocean_next: bfloat16 [384, 768, 256], P('band', ('comp', 'tile'))
- surface_fields: float32 [384, 768, 4], P('band', ('comp', 'tile'))
All inputs are finite; a program needn't handle non-finite values. No bound on the sum of `sea_mask` on one device may be relied on, other than what follows from the above.
Results may differ from a plain program's by a relative error of at most 0.0095.
Values may be sent and summed in bfloat16 or wider, within the bound.
A program may use at most 128 MiB of HBM per device.

v0:
```python
import functools
import math

import jax
import jax.numpy as jnp
import numpy as np
from jax import lax
from jax.experimental import pallas as pl
from jax.experimental.pallas import tpu as pltpu
from jax.sharding import PartitionSpec as P

MESH = pl.DeviceIdType.MESH
full_precision = lax.Precision.HIGHEST
eps_norm = 1e-06
shrink_level = 0.01


def with_halo(cells, sides, width, closed):
    for axis, dim in sides:
        count = lax.axis_size(axis)
        ends = count if closed else count - 1
        head = lax.slice_in_dim(cells, 0, width, axis=dim)
        tail = lax.slice_in_dim(cells, cells.shape[dim] - width, cells.shape[dim], axis=dim)
        cells = jnp.concatenate(
            [
                lax.ppermute(tail, axis, [(i, (i + 1) % count) for i in range(ends)]),
                cells,
                lax.ppermute(head, axis, [((i + 1) % count, i) for i in range(ends)]),
            ],
            axis=dim,
        )
    return cells


def layer_norm(values, scaling, offset):
    average = jnp.mean(values, axis=-1, keepdims=True)
    squares = jnp.mean(values * values, axis=-1, keepdims=True)
    variance = squares - average * average
    return (values - average) * lax.rsqrt(variance + eps_norm) * scaling + offset


def soft_shrink(values):
    zeros = jnp.zeros_like(values)
    return jnp.where(
        values > shrink_level,
        values - shrink_level,
        jnp.where(values < -shrink_level, values + shrink_level, zeros),
    )


def channel_mlp(tokens, layer_index, norm_gain, norm_shift, w_in, w_out):
    flat_tokens = tokens.reshape(-1, tokens.shape[-1]).astype(jnp.float32)
    second = layer_norm(flat_tokens, norm_gain[layer_index, 1], norm_shift[layer_index, 1]).astype(
        jnp.bfloat16
    )
    hidden = jax.nn.gelu(
        jnp.dot(second, w_in, preferred_element_type=jnp.float32), approximate=False
    ).astype(jnp.bfloat16)
    summed = jnp.dot(hidden, w_out, preferred_element_type=jnp.float32)
    return (flat_tokens + summed).astype(jnp.bfloat16).reshape(tokens.shape)


def split_bf16(array):
    high = array.astype(jnp.bfloat16)
    return high, (array - high.astype(jnp.float32)).astype(jnp.bfloat16)


def host_split(array):
    whole = np.asarray(array, np.float32)
    high = whole.astype(jnp.bfloat16)
    low = (whole - high.astype(np.float32)).astype(jnp.bfloat16)
    return jnp.asarray(np.stack([high, low]))


def transforms(latitudes, longitudes, bands):
    kept = longitudes // 2
    each, rows = kept // bands, latitudes // bands
    waves = np.arange(kept).reshape(bands, each).T.reshape(-1)
    lats = np.arange(latitudes).reshape(bands, rows).T.reshape(-1)
    lon = np.outer(waves, np.arange(longitudes)) % longitudes * (2.0 * math.pi / longitudes)
    lat = np.outer(np.arange(latitudes), lats) % latitudes * (2.0 * math.pi / latitudes)
    forward = np.concatenate([np.cos(lon), -np.sin(lon)], 0) / math.sqrt(longitudes)
    across = np.stack([np.cos(lat), np.sin(lat)], 0) / math.sqrt(latitudes)
    weight = np.where(waves == 0, 1.0, 2.0)[:, None]
    inverse = np.concatenate([np.cos(lon) * weight, -np.sin(lon) * weight], 0).T
    return (
        host_split(forward),
        host_split(across.reshape(2 * latitudes, latitudes)),
        host_split(across.transpose(0, 2, 1).reshape(2 * latitudes, latitudes)),
        host_split(inverse / math.sqrt(longitudes)),
    )


def mix_matrices(weights, biases):
    slot, width = weights.shape[-2:]
    groups = slot // width
    eye = jnp.eye(groups, dtype=weights.dtype)
    full = weights.reshape(2, 2, groups, width, 1, width) * eye[None, None, :, None, :, None]
    full = full.reshape(2, 2, slot, slot)
    whole = jnp.concatenate(
        [
            jnp.concatenate([full[:, 0], full[:, 1]], axis=2),
            jnp.concatenate([-full[:, 1], full[:, 0]], axis=2),
        ],
        axis=1,
    )
    def lanes(array, axis):
        part = [lax.slice_in_dim(array, a, b, axis=axis) for a, b in
                ((0, 128), (slot, slot + 128), (128, slot), (slot + 128, 2 * slot))]
        return jnp.concatenate(part, axis=axis)
    whole = lanes(lanes(whole, 1), 2)
    high, low = split_bf16(whole)
    offsets = lanes(biases.reshape(2, 2 * slot), 1)
    return jnp.stack([high, low], axis=1), jnp.concatenate([offsets, jnp.zeros((6, 2 * slot))], 0)


def product(left, right):
    total = None
    for a, b in ((0, 0), (1, 0), (0, 1)):
        if a < len(left) and b < len(right):
            term = jnp.dot(left[a], right[b], preferred_element_type=jnp.float32)
            total = term if total is None else total + term
    return total


def filter_kernel(
    bands, exchanged, x_ref, affine_ref, forward_ref, across_ref, back_ref, inverse_ref, mix_ref,
    offset_ref, out_ref, *scratch
):
    if exchanged:
        held, scratch = scratch[0], scratch[1:]
    (
        normed, after, stage, landed, sums, all_sums, send_a, got_a, send_b, got_b,
        sent_team, came_team, sent_sum, came_sum, sent_a, came_a, sent_b, came_b, sent_out, came_out,
    ) = scratch
    rows, quarter, slot = out_ref.shape[1:]
    longitudes = 4 * quarter
    latitudes = rows * bands
    each = longitudes // 2 // bands
    me = lax.axis_index("band")
    mine = lax.axis_index("comp") * 2 + lax.axis_index("tile")

    def member(step):
        return lax.rem(mine + step, 4)

    def team_id(index):
        return {"comp": lax.div(index, 2), "tile": lax.rem(index, 2)}

    barrier = pltpu.get_barrier_semaphore()

    def greet(step, carry):
        pl.semaphore_signal(
            barrier, inc=1, device_id={"band": lax.rem(me + step, bands)}, device_id_type=MESH
        )
        return carry

    for step in range(1, 4):
        pl.semaphore_signal(barrier, inc=1, device_id=team_id(member(step)), device_id_type=MESH)
    lax.fori_loop(1, bands, greet, 0)

    def team_copy(source, target, sent, came, step, whole=False):
        index = member(step)
        return pltpu.make_async_remote_copy(
            src_ref=source if whole else source.at[index],
            dst_ref=target.at[mine],
            send_sem=sent.at[index],
            recv_sem=came.at[mine],
            device_id=team_id(index),
            device_id_type=MESH,
        )

    def team_landing(source, target, sent, came, step, whole=False):
        index = member(step)
        return pltpu.make_async_remote_copy(
            src_ref=source if whole else source.at[index],
            dst_ref=target.at[index],
            send_sem=sent.at[index],
            recv_sem=came.at[index],
            device_id=team_id(index),
            device_id_type=MESH,
        )

    def team_exchange(*args):
        for step in range(1, 4):
            team_copy(*args[:4], step, *args[4:]).start()

    def team_finish(*args):
        for step in range(1, 4):
            team_landing(*args[:4], step, *args[4:]).wait()

    if exchanged:
        pl.semaphore_wait(barrier, bands - 1 + 3)
        team_exchange(x_ref, held, sent_team, came_team)
        held[mine] = x_ref[mine]
        team_finish(x_ref, held, sent_team, came_team)

    def tokens(lat):
        if exchanged:
            return jnp.concatenate([held[s, lat] for s in range(4)], axis=0)
        return x_ref[lat]

    ones = jnp.ones((8, slot), jnp.bfloat16)
    which = lax.broadcasted_iota(jnp.int32, (8, longitudes), 0)
    turned = (((1,), (1,)), ((), ()))

    def row_sum(values):
        return lax.dot_general(ones, values, turned, preferred_element_type=jnp.float32)

    total = jnp.zeros((8, longitudes), jnp.float32)
    for lat in range(rows):
        values = tokens(lat)
        wide = values.astype(jnp.float32)
        high, low = split_bf16(wide * wide)
        total = total + jnp.where(which == lat, row_sum(values), 0.0)
        total = total + jnp.where(which == rows + lat, row_sum(high) + row_sum(low), 0.0)
    sums[...] = total
    if not exchanged:
        pl.semaphore_wait(barrier, bands - 1 + 3)
    team_exchange(sums, all_sums, sent_sum, came_sum, True)
    all_sums[mine] = total
    team_finish(sums, all_sums, sent_sum, came_sum, True)
    total = (all_sums[0] + all_sums[1] + all_sums[2] + all_sums[3]) * (1.0 / (4 * slot))
    columns = jnp.concatenate([total, jnp.zeros((120, longitudes), jnp.float32)], axis=0).T

    lane = lax.broadcasted_iota(jnp.int32, (1, 128), 1)
    first_half = lane < slot - 128
    sign = jnp.where(first_half, 1.0, -1.0)
    half = longitudes // 2

    def spread(lat, wave, part, values):
        stage[pl.ds(part * 9 + lat * 3 + wave, bands, stride=32), :] = values

    def collect(lat, wave, part):
        return landed[pl.ds(part * 9 + lat * 3 + wave, bands, stride=32), :]

    for lat in range(rows):
        values = tokens(lat).astype(jnp.float32)
        average = columns[:, lat : lat + 1]
        second = columns[:, rows + lat : rows + lat + 1]
        scaled = (values - average) * lax.rsqrt(second - average * average + eps_norm)
        scaled = scaled * affine_ref[0:1, :] + affine_ref[1:2, :]
        normed[lat] = scaled
        tail = scaled[:, 128:]
        wide = jnp.concatenate([scaled[:, :128], tail, tail], axis=1)
        spectrum = product((forward_ref[0], forward_ref[1]), split_bf16(wide))
        upper, lower = spectrum[:half], spectrum[half:]
        parts = (upper[:, :128], lower[:, :128], jnp.where(first_half, upper[:, 128:], lower[:, 128:]))
        for part in range(3):
            for wave in range(each):
                spread(lat, wave, part, parts[part][wave * bands : (wave + 1) * bands])

    def band_copy(source, target, sent, came, step, landing):
        index = lax.rem(me + step, bands)
        return pltpu.make_async_remote_copy(
            src_ref=source.at[index],
            dst_ref=target.at[index if landing else me],
            send_sem=sent.at[index],
            recv_sem=came.at[index if landing else me],
            device_id={"band": index},
            device_id_type=MESH,
        )

    def band_exchange(source, target, sent, came):
        source[...] = stage[...].astype(jnp.bfloat16).reshape(source.shape)

        def go(step, carry):
            band_copy(source, target, sent, came, step, False).start()
            return carry

        lax.fori_loop(1, bands, go, 0)
        target[me] = source[me]

        def come(step, carry):
            band_copy(source, target, sent, came, step, True).wait()
            return carry

        lax.fori_loop(1, bands, come, 0)
        landed[...] = target[...].astype(jnp.float32).reshape(landed.shape)

    band_exchange(send_a, got_a, sent_a, came_a)
    pieces = []
    for wave in range(each):
        for part in range(3):
            pieces.append(
                jnp.concatenate([collect(lat, wave, part) for lat in range(rows)], axis=0)
            )
    spectrum = jnp.concatenate(pieces, axis=1).astype(jnp.bfloat16)
    turned_all = product((across_ref[0], across_ref[1]), (spectrum,))

    def combine(both, wave, direction):
        base = wave * 384
        cosine, sine = both[:latitudes, base : base + 384], both[latitudes:, base : base + 384]
        real = cosine[:, :128] + direction * sine[:, 128:256]
        imag = cosine[:, 128:256] - direction * sine[:, :128]
        rest = cosine[:, 256:] + (direction * sign) * pltpu.roll(sine[:, 256:], 64, 1)
        return real, imag, rest

    rows_in = jnp.concatenate(
        [jnp.concatenate(combine(turned_all, wave, 1.0), axis=1) for wave in range(each)], axis=0
    )
    hidden = product(split_bf16(rows_in), (mix_ref[0, 0], mix_ref[0, 1])) + offset_ref[0:1, :]
    hidden = jnp.maximum(hidden, 0.0)
    mixed = product(split_bf16(hidden), (mix_ref[1, 0], mix_ref[1, 1])) + offset_ref[1:2, :]
    mixed = soft_shrink(mixed)
    columns_back = jnp.concatenate(
        [mixed[wave * latitudes : (wave + 1) * latitudes] for wave in range(each)], axis=1
    )
    turned_back = product((back_ref[0], back_ref[1]), split_bf16(columns_back))
    for wave in range(each):
        parts = combine(turned_back, wave, -1.0)
        for part in range(3):
            for lat in range(rows):
                spread(lat, wave, part, parts[part][lat * bands : (lat + 1) * bands])
    band_exchange(send_b, got_b, sent_b, came_b)
    for lat in range(rows):
        real, imag, rest = (
            jnp.concatenate([collect(lat, wave, part) for wave in range(each)], axis=0)
            for part in range(3)
        )
        right = jnp.concatenate(
            [
                jnp.concatenate([real, rest], axis=1),
                jnp.concatenate([imag, pltpu.roll(rest, 64, 1)], axis=1),
            ],
            axis=0,
        ).astype(jnp.bfloat16)
        restored = product((inverse_ref[0], inverse_ref[1]), (right,))
        result = tokens(lat).astype(jnp.float32) + restored[:, :slot] + normed[lat]
        result = result.astype(jnp.bfloat16)
        for s in range(4):
            after[s, lat] = result[s * quarter : (s + 1) * quarter]
    team_exchange(after, out_ref, sent_out, came_out)
    out_ref[mine] = after[mine]
    team_finish(after, out_ref, sent_out, came_out)


def spectral_filter(values, gain, shift, weights, biases, bands, exchanged):
    if exchanged:
        quarter, slot = values.shape[2:]
        rows, longitudes = values.shape[1], 4 * quarter
    else:
        rows, longitudes, slot = values.shape
        quarter = longitudes // 4
    latitudes = rows * bands
    mats = transforms(latitudes, longitudes, bands)
    mix, offsets = mix_matrices(weights, biases)
    affine = jnp.concatenate([gain[None], shift[None], jnp.zeros((6, slot))], 0)
    team = pltpu.VMEM((4, rows, quarter, slot), jnp.bfloat16)
    chunks = pltpu.VMEM((bands, 32, 128), jnp.bfloat16)
    four = pltpu.SemaphoreType.DMA((4,))
    many = pltpu.SemaphoreType.DMA((bands,))
    scratch = [team] if exchanged else []
    scratch += [
        pltpu.VMEM((rows, longitudes, slot), jnp.float32),
        team,
        pltpu.VMEM((bands * 32, 128), jnp.float32),
        pltpu.VMEM((bands * 32, 128), jnp.float32),
        pltpu.VMEM((8, longitudes), jnp.float32),
        pltpu.VMEM((4, 8, longitudes), jnp.float32),
        chunks, chunks, chunks, chunks,
        four, four, four, four, many, many, many, many, four, four,
    ]
    return pl.pallas_call(
        functools.partial(filter_kernel, bands, exchanged),
        out_shape=jax.ShapeDtypeStruct((4, rows, quarter, slot), jnp.bfloat16),
        in_specs=[pl.BlockSpec(memory_space=pltpu.VMEM)] * 8,
        out_specs=pl.BlockSpec(memory_space=pltpu.VMEM),
        scratch_shapes=scratch,
        compiler_params=pltpu.CompilerParams(
            collective_id=1 if exchanged else 0, has_side_effects=True, vmem_limit_bytes=60 << 20
        ),
    )(values, affine, *mats, mix, offsets)


def on_device(
    atmosphere,
    spec_weight,
    spec_bias,
    norm_gain,
    norm_shift,
    fc_in,
    fc_out,
    flux_head,
    flux_embed,
    ocean_state,
    sea_mask,
    depth_kernel,
    ocean_gain,
    ocean_shift,
    ocean_in,
    ocean_out,
    layer_scale,
    field_head,
    patch_embed,
):
    column_index = lax.axis_index(("comp", "tile"))
    team = ("comp", "tile")
    slot = atmosphere.shape[-1]
    w_in = [lax.all_gather(fc_in[b], team, axis=1, tiled=True) for b in range(2)]
    w_out = [lax.all_gather(fc_out[b], team, axis=0, tiled=True) for b in range(2)]
    head = lax.all_gather(flux_head, team, axis=0, tiled=True)
    embed = lax.all_gather(patch_embed, team, axis=1, tiled=True)

    bands = lax.axis_size("band")

    def filtered(values, block):
        gain = lax.dynamic_slice_in_dim(norm_gain[block, 0], column_index * slot, slot)
        shift = lax.dynamic_slice_in_dim(norm_shift[block, 0], column_index * slot, slot)
        pieces = spectral_filter(
            values, gain, shift, spec_weight[block], spec_bias[block], bands, block == 1
        )
        return pieces.transpose(1, 2, 0, 3).reshape(pieces.shape[1], pieces.shape[2], -1)

    tokens = filtered(atmosphere, 0)
    after_one = channel_mlp(tokens, 0, norm_gain, norm_shift, w_in[0], w_out[0])
    fluxes = jnp.einsum("lnc,cf->lnf", after_one, head, preferred_element_type=jnp.float32)
    upsampled = jnp.repeat(jnp.repeat(fluxes, 2, axis=0), 2, axis=1)
    sea_cells = sea_mask.astype(jnp.float32)[..., None]
    forcing = jnp.einsum("ijf,fc->ijc", upsampled, flux_embed, precision=full_precision)
    start = (ocean_state.astype(jnp.float32) + sea_cells * forcing).astype(jnp.bfloat16)
    widened = with_halo(start, ((("comp", "tile"), 1),), 3, True)
    extended = with_halo(widened, (("band", 0),), 3, False).astype(jnp.float32)
    tile_rows = start.shape[0]
    tile_columns = start.shape[1]
    convolved = jnp.zeros(start.shape, jnp.float32)
    for row_step in range(7):
        for col_step in range(7):
            convolved = (
                convolved
                + extended[row_step : row_step + tile_rows, col_step : col_step + tile_columns]
                * depth_kernel[row_step, col_step]
            )
    normed = layer_norm(convolved, ocean_gain, ocean_shift).astype(jnp.bfloat16)
    flat_cells = normed.reshape(-1, normed.shape[-1])
    hidden = jax.nn.gelu(
        jnp.dot(flat_cells, ocean_in, preferred_element_type=jnp.float32), approximate=False
    ).astype(jnp.bfloat16)
    update = jnp.dot(hidden, ocean_out, preferred_element_type=jnp.float32).reshape(start.shape)
    ocean_next = (start.astype(jnp.float32) + sea_cells * layer_scale * update).astype(jnp.bfloat16)
    surface = sea_cells * jnp.einsum(
        "ijc,cf->ijf", ocean_next.astype(jnp.float32), field_head, precision=full_precision
    )
    half_rows = tile_rows // 2
    half_columns = tile_columns // 2
    patches = (
        surface.reshape(half_rows, 2, half_columns, 2, surface.shape[2])
        .transpose(0, 2, 4, 1, 3)
        .reshape(half_rows, half_columns, -1)
    )
    embedding = jnp.einsum("pqk,kd->pqd", patches, embed, precision=full_precision)
    middle = (after_one.astype(jnp.float32) + embedding).astype(jnp.bfloat16)
    pieces = middle.reshape(middle.shape[0], middle.shape[1], 4, slot).transpose(2, 0, 1, 3)
    tokens = filtered(pieces, 1)
    result = channel_mlp(tokens, 1, norm_gain, norm_shift, w_in[1], w_out[1])
    atmosphere_next = lax.all_to_all(result, team, split_axis=2, concat_axis=1, tiled=True)
    return (atmosphere_next, ocean_next, surface)


def solution(mesh):
    placed = (
        P("band", None, ("comp", "tile")),
        P(None, None, None, ("comp", "tile"), None),
        P(None, None, None, ("comp", "tile")),
        P(),
        P(),
        P(None, None, ("comp", "tile")),
        P(None, ("comp", "tile"), None),
        P(("comp", "tile"), None),
        P(),
        P("band", ("comp", "tile"), None),
        P("band", ("comp", "tile")),
        P(),
        P(),
        P(),
        P(),
        P(),
        P(),
        P(),
        P(None, ("comp", "tile")),
    )
    return jax.shard_map(
        on_device,
        mesh=mesh,
        in_specs=placed,
        out_specs=(
            P("band", None, ("comp", "tile")),
            P("band", ("comp", "tile"), None),
            P("band", ("comp", "tile"), None),
        ),
        check_vma=False,
    )
```

profile of v0, /device:TPU:1, one launch (start us, length us, event | category | flops | bytes accessed | tf_op | source)
XLA Modules:
  0.0 310.6 jit_solution(10006762525302598462)
XLA Ops:
  7.2 3.5 %fusion.305 = (bf16[1,768,768]{2,1,0:T(8,128)(2,1)}, bf16[1,768,768]{2,1,0:T(8,128)(2,1)}) fusion(bf16[2,768,768]{2,1,0:T(8,128)(2,1)} %param.32), kind=kLoop, calls=%fused_computation.422 | loop fusion | bytes 4718592 | tf_op jit(solution)/shard_map/slice | solution.py:399
  10.8 1.6 fusion.306
  19.8 1.2 copy.76.mix_ref
  24.8 78.5 %shard_map.274 = bf16[4,3,96,192]{3,2,1,0:T(8,128)(2,1)} custom-call(bf16[3,384,192]{2,1,0:T(8,128)(2,1)} %copy.75.x_ref, f32[8,192]{1,0:T(8,128)} %get-tuple-element.112.affine_ref, bf16[2,384,384]{2,1,0:T(8,128)(2,1)} %constant.20.clone.forward_ref, bf16[2,384,192]{2,1,0:T(8,128)(2,1)} %constant.21.clone.across_ref, ...), custom_call_target="tpu_custom_call" | custom-call | tf_op jit(solution)/shard_map/pallas_call | solution.py:363
  103.3 1.4 fusion.185
  104.7 1.2 convert_bitcast_fusion.1
  109.5 1.7 reshape.416
  111.2 6.0 %all-gather.4 = bf16[4,192,8]{1,2,0:T(8,128)(2,1)S(1)} all-gather(bf16[1,192,8]{1,2,0:T(8,128)(2,1)S(1)} %bitcast.241), channel_id=1, replica_groups=mesh['band'=64,'comp'=2,'tile'=2] {'comp','tile'}, dimensions={0}, use_global_device_ids=true | all-gather | bytes 15360 | tf_op jit(solution)/shard_map/all_gather | solution.py:401
  117.3 1.2 pad_maximum_fusion.3.mix_ref
  118.7 13.8 %fusion.119 = bf16[288,768]{1,0:T(8,128)(2,1)S(1)} fusion(f32[288,768]{1,0:T(8,128)S(1)} %copy-done.5, bf16[1,3072,768]{2,1,0:T(8,128)(2,1)} %all-gather.13.cloned.1.call-done, bf16[1,768,3072]{2,1,0:T(8,128)(2,1)} %all-gather.11.cloned.1.call-done, f32[768]{0:T(1024)S(1)} %get-tuple-element.97, f32[768]{0:T(1024)S(1)} %get-tuple-element.93, ...), kind=kOutput, calls=%fused_computation.136 | convolution fusion | flops 2776965120 | bytes 10772736 | tf_op jit(solution)/shard_map/dot_general | solution.py:59
  134.7 2.0 collective-permute-start
  136.7 8.7 %all-gather.5 = f32[4,192,16]{1,2,0:T(8,128)S(1)} all-gather(f32[1,192,16]{1,2,0:T(8,128)S(1)} %bitcast.191), channel_id=1, replica_groups=mesh['band'=64,'comp'=2,'tile'=2] {'comp','tile'}, dimensions={0}, use_global_device_ids=true | all-gather | bytes 61440 | tf_op jit(solution)/shard_map/all_gather | solution.py:402
  145.8 2.3 collective-permute-start.2
  148.1 1.3 collective-permute-start.3
  151.4 3.1 %collective-permute-done.2 = bf16[3,198,256]{2,1,0:T(8,128)(2,1)S(1)} collective-permute-done((bf16[3,198,256]{2,1,0:T(8,128)(2,1)S(1)}, bf16[3,198,256]{2,1,0:T(8,128)(2,1)S(1)}, u32[]{:S(2)}, u32[]{:S(2)}) %collective-permute-start.2) | collective-permute-done | bytes 304160 | tf_op jit(solution)/shard_map/ppermute | solution.py:26
  154.6 4.0 %collective-permute-done.3 = bf16[3,198,256]{2,1,0:T(8,128)(2,1)S(1)} collective-permute-done((bf16[3,198,256]{2,1,0:T(8,128)(2,1)S(1)}, bf16[3,198,256]{2,1,0:T(8,128)(2,1)S(1)}, u32[]{:S(2)}, u32[]{:S(2)}) %collective-permute-start.3) | collective-permute-done | bytes 304160 | tf_op jit(solution)/shard_map/ppermute | solution.py:28
  159.0 9.1 %fusion.303 = (f32[6,192]{1,0:T(8,128)S(1)}, f32[6,192]{1,0:T(8,128)S(1)}, f32[6,192,256]{2,1,0:T(8,128)S(1)}) fusion(f32[256]{0:T(256)S(1)} %bitcast.220, f32[12,198,256]{2,1,0:T(8,128)S(1)} %maximum_convert_fusion, f32[256]{0:T(256)S(1)} %bitcast.221, f32[256]{0:T(256)S(1)} %bitcast.193, f32[256]{0:T(256)S(1)} %bitcast.194, f32[256]{0:T(256)S(1)} %bitcast.195, ...), kind=kLoop, calls=%fused_computation.421 | loop fusion | flops 29488896 | bytes 59041792 | tf_op jit(solution)/shard_map/reduce_sum | solution.py:36
  168.6 11.8 %fusion.101 = f32[1152,256]{1,0:T(8,128)S(1)} fusion(bf16[1024,256]{1,0:T(8,128)(2,1)S(1)} %copy-done, bf16[1152,256]{1,0:T(8,128)(2,1)S(1)} %bitcast.188, bf16[256,1024]{1,0:T(8,128)(2,1)} %param.41), kind=kOutput, calls=%fused_computation.129 | convolution fusion | flops 1284636672 | bytes 2818048 | tf_op jit(solution)/shard_map/dot_general | solution.py:438
  184.8 83.0 %shard_map.275 = bf16[4,3,96,192]{3,2,1,0:T(8,128)(2,1)} custom-call(bf16[4,3,96,192]{3,2,1,0:T(8,128)(2,1)} %bitcast.179, f32[8,192]{1,0:T(8,128)} %get-tuple-element.111.affine_ref, bf16[2,384,384]{2,1,0:T(8,128)(2,1)} %constant.20.clone.forward_ref, bf16[2,384,192]{2,1,0:T(8,128)(2,1)} %constant.21.clone.across_ref, ...), custom_call_target="tpu_custom_call" | custom-call | tf_op jit(solution)/shard_map/pallas_call | solution.py:363
  267.8 1.4 fusion.186
  269.4 1.2 convert_bitcast_fusion
  272.2 14.1 %fusion.114 = bf16[288,768]{1,0:T(8,128)(2,1)S(1)} fusion(f32[288,768]{1,0:T(8,128)S(1)} %reshape.417, bf16[1,3072,768]{2,1,0:T(8,128)(2,1)} %all-gather.17.cloned.1.call-done, bf16[1,768,3072]{2,1,0:T(8,128)(2,1)} %all-gather.15.cloned.1.call-done, f32[768]{0:T(1024)S(1)} %copy-done.47, f32[768]{0:T(1024)S(1)} %copy-done.48, f32[288]{0:T(512)S(1)} %add_rsqrt_fusion.1, ...), kind=kOutput, calls=%fused_computation.135 | convolution fusion | flops 2776965120 | bytes 10772736 | tf_op jit(solution)/shard_map/dot_general | solution.py:59
  286.9 15.0 %all_to_all.18 = bf16[3,96,768]{1,0,2:T(4,128)(2,1)S(1)} all-to-all(bf16[3,96,768]{1,0,2:T(4,128)(2,1)S(1)} %copy.90), channel_id=1, replica_groups=mesh['band'=64,'comp'=2,'tile'=2] {'comp','tile'}, dimensions={2} | all-to-all | bytes 884736 | tf_op jit(solution)/shard_map/all_to_all | solution.py:455
  302.4 1.2 all_to_all.16
  (202 shorter events, 27.3 us)
Async XLA Ops:
  7.2 161.4 %copy-start = (bf16[1024,256]{1,0:T(8,128)(2,1)S(1)}, bf16[1024,256]{1,0:T(8,128)(2,1)}, u32[]{:S(2)}) copy-start(bf16[1024,256]{1,0:T(8,128)(2,1)} %param.42) | copy-start | bytes 1572868
  7.2 111.4 %all-gather.11.cloned.1.call-start = ((), (), s32[]{:S(2)}) async-start(), calls=%async_computation.1 | async-start | bytes 5898240 | tf_op jit(solution)/shard_map/all_gather | solution.py:399
  10.7 107.8 %all-gather.13.cloned.1.call-start = ((), (), s32[]{:S(2)}) async-start(), calls=%async_computation.2 | async-start | bytes 5898240 | tf_op jit(solution)/shard_map/all_gather | solution.py:400
  12.4 259.8 %all-gather.15.cloned.1.call-start = ((), (), s32[]{:S(2)}) async-start(), calls=%async_computation.3 | async-start | bytes 5898240 | tf_op jit(solution)/shard_map/all_gather | solution.py:399
  13.1 259.1 %all-gather.17.cloned.1.call-start = ((), (), s32[]{:S(2)}) async-start(), calls=%async_computation.4 | async-start | bytes 5898240 | tf_op jit(solution)/shard_map/all_gather | solution.py:400
  109.5 7.8 %copy-start.16 = (s32[6,192]{1,0:T(8,128)S(1)}, s32[6,192]{1,0:T(8,128)}, u32[]{:S(2)}) copy-start(s32[6,192]{1,0:T(8,128)} %param.37) | copy-start | bytes 13828
  109.5 7.8 %copy-start.4 = (bf16[2,1,384,384]{3,2,1,0:T(8,128)(2,1)S(1)}, bf16[2,1,384,384]{3,2,1,0:T(8,128)(2,1)}, u32[]{:S(2)}) copy-start(bf16[2,1,384,384]{3,2,1,0:T(8,128)(2,1)} %subtract_convert_fusion) | copy-start | bytes 1769476
  134.7 10.9 %collective-permute-start = (bf16[6,3,256]{2,1,0:T(4,128)(2,1)S(1)}, bf16[6,3,256]{2,1,0:T(4,128)(2,1)S(1)}, u32[]{:S(2)}, u32[]{:S(2)}) collective-permute-start(bf16[6,3,256]{2,1,0:T(4,128)(2,1)S(1)} %get-tuple-element.34), channel_id=1, source_target_pairs={{0,1},{1,2},{2,3},{3,0},{4,5},{5,6},{6,7},{7,4},{8,9},{9,10},{10,1... | collective-permute-start | bytes 27656 | tf_op jit(solution)/shard_map/ppermute | solution.py:26
  136.7 8.9 %collective-permute-start.1 = (bf16[6,3,256]{2,1,0:T(4,128)(2,1)S(1)}, bf16[6,3,256]{2,1,0:T(4,128)(2,1)S(1)}, u32[]{:S(2)}, u32[]{:S(2)}) collective-permute-start(bf16[6,3,256]{2,1,0:T(4,128)(2,1)S(1)} %get-tuple-element.35), channel_id=1, source_target_pairs={{1,0},{2,1},{3,2},{0,3},{5,4},{6,5},{7,6},{4,7},{9,8},{10,9},{11,1... | collective-permute-start | bytes 27656 | tf_op jit(solution)/shard_map/ppermute | solution.py:28
  145.8 8.7 %collective-permute-start.2 = (bf16[3,198,256]{2,1,0:T(8,128)(2,1)S(1)}, bf16[3,198,256]{2,1,0:T(8,128)(2,1)S(1)}, u32[]{:S(2)}, u32[]{:S(2)}) collective-permute-start(bf16[3,198,256]{2,1,0:T(8,128)(2,1)S(1)} %get-tuple-element.32), channel_id=1, source_target_pairs={{0,4},{4,8},{8,12},{12,16},{16,20},{20,24},{24,28},{28,32},{32,36}... | collective-permute-start | bytes 912392 | tf_op jit(solution)/shard_map/ppermute | solution.py:26
  148.1 10.4 %collective-permute-start.3 = (bf16[3,198,256]{2,1,0:T(8,128)(2,1)S(1)}, bf16[3,198,256]{2,1,0:T(8,128)(2,1)S(1)}, u32[]{:S(2)}, u32[]{:S(2)}) collective-permute-start(bf16[3,198,256]{2,1,0:T(8,128)(2,1)S(1)} %get-tuple-element.33), channel_id=1, source_target_pairs={{4,0},{8,4},{12,8},{16,12},{20,16},{24,20},{28,24},{32,28},{36,32}... | collective-permute-start | bytes 912392 | tf_op jit(solution)/shard_map/ppermute | solution.py:28
  151.2 7.6 %copy-start.18 = (f32[1,1,256]{2,1,0:T(1,128)S(1)}, f32[1,1,256]{2,1,0:T(1,128)}, u32[]{:S(2)}) copy-start(f32[1,1,256]{2,1,0:T(1,128)} %get-tuple-element.48) | copy-start | bytes 3076
  151.2 7.6 %copy-start.19 = (f32[1,1,256]{2,1,0:T(1,128)S(1)}, f32[1,1,256]{2,1,0:T(1,128)}, u32[]{:S(2)}) copy-start(f32[1,1,256]{2,1,0:T(1,128)} %get-tuple-element.49) | copy-start | bytes 3076
  151.2 7.6 %copy-start.20 = (f32[1,1,256]{2,1,0:T(1,128)S(1)}, f32[1,1,256]{2,1,0:T(1,128)}, u32[]{:S(2)}) copy-start(f32[1,1,256]{2,1,0:T(1,128)} %get-tuple-element.50) | copy-start | bytes 3076
  151.2 7.6 %copy-start.21 = (f32[1,1,256]{2,1,0:T(1,128)S(1)}, f32[1,1,256]{2,1,0:T(1,128)}, u32[]{:S(2)}) copy-start(f32[1,1,256]{2,1,0:T(1,128)} %get-tuple-element.51) | copy-start | bytes 3076
  151.2 7.6 %copy-start.22 = (f32[1,1,256]{2,1,0:T(1,128)S(1)}, f32[1,1,256]{2,1,0:T(1,128)}, u32[]{:S(2)}) copy-start(f32[1,1,256]{2,1,0:T(1,128)} %get-tuple-element.52) | copy-start | bytes 3076
  151.2 7.6 %copy-start.23 = (f32[1,1,256]{2,1,0:T(1,128)S(1)}, f32[1,1,256]{2,1,0:T(1,128)}, u32[]{:S(2)}) copy-start(f32[1,1,256]{2,1,0:T(1,128)} %get-tuple-element.53) | copy-start | bytes 3076
  151.2 7.6 %copy-start.24 = (f32[1,1,256]{2,1,0:T(1,128)S(1)}, f32[1,1,256]{2,1,0:T(1,128)}, u32[]{:S(2)}) copy-start(f32[1,1,256]{2,1,0:T(1,128)} %get-tuple-element.54) | copy-start | bytes 3076
  151.2 7.6 %copy-start.25 = (f32[1,1,256]{2,1,0:T(1,128)S(1)}, f32[1,1,256]{2,1,0:T(1,128)}, u32[]{:S(2)}) copy-start(f32[1,1,256]{2,1,0:T(1,128)} %get-tuple-element.55) | copy-start | bytes 3076
  151.3 7.6 %copy-start.26 = (f32[1,1,256]{2,1,0:T(1,128)S(1)}, f32[1,1,256]{2,1,0:T(1,128)}, u32[]{:S(2)}) copy-start(f32[1,1,256]{2,1,0:T(1,128)} %get-tuple-element.56) | copy-start | bytes 3076
  151.3 7.6 %copy-start.27 = (f32[1,1,256]{2,1,0:T(1,128)S(1)}, f32[1,1,256]{2,1,0:T(1,128)}, u32[]{:S(2)}) copy-start(f32[1,1,256]{2,1,0:T(1,128)} %get-tuple-element.57) | copy-start | bytes 3076
  159.0 9.2 %copy-start.49 = (f32[256]{0:T(256)S(1)}, f32[256]{0:T(256)}, u32[]{:S(2)}) copy-start(f32[256]{0:T(256)} %param.40) | copy-start | bytes 3076
  159.0 9.2 %copy-start.50 = (f32[256]{0:T(256)S(1)}, f32[256]{0:T(256)}, u32[]{:S(2)}) copy-start(f32[256]{0:T(256)} %param.39) | copy-start | bytes 3076
  168.6 11.8 %copy-start.51 = (f32[256]{0:T(256)S(1)}, f32[256]{0:T(256)}, u32[]{:S(2)}) copy-start(f32[256]{0:T(256)} %param.43) | copy-start | bytes 3076
  (36 other events, 152.4 us)
Sparse Core Ops, SparseCore 0:
  10.8 54.3 all-gather.10
  67.1 49.7 all-gather.12
  118.7 50.4 all-gather.14
  170.9 47.9 all-gather.16
where the time goes:
time: 316 us; the launch traced here: 311 us
  Pallas kernels  162 us (51%)
  matrix products  42.6 us (13%)
  blocking collectives  29.7 us (9%)
  local copies, waits for them, and re-layouts  26.3 us (8%)
  other arithmetic  21 us (7%)
  between operations  15.4 us (5%)
  waiting for transfers between devices  8.37 us (3%)
  starting transfers between devices  5.72 us (2%)
    pallas_call x2, Pallas kernels, spectral_filter(): pl.pallas_call(functools.partial(filter_kernel, bands, exchanged), out_sh...  162 us
    dot_general x2, matrix products, channel_mlp(): summed = jnp.dot(hidden, w_out, preferred_element_type=jnp.float32)  27.8 us
    all_to_all x1, blocking collectives, on_device(): lax.all_to_all(result, team, split_axis=2, concat_axis=1, tiled=True)  15 us
    reduce_sum x3, other arithmetic, layer_norm(): average = jnp.mean(values, axis=-1, keepdims=True)  11.8 us
    dot_general x1, matrix products, on_device(): jnp.dot(hidden, ocean_out, preferred_element_type=jnp.float32)  11.8 us
    all_gather x1, blocking collectives, on_device(): embed = lax.all_gather(patch_embed, team, axis=1, tiled=True)  8.72 us
  transfers between devices with their start and end apart: 8, of which 2 were waited for; matrix products, arithmetic and copies ran while one was open for 22% of the time, Pallas kernels for 52%

commit v1 on v0

v1 whole, which is shorter than its diff:
```python
import functools
import math

import jax
import jax.numpy as jnp
import numpy as np
from jax import lax
from jax.experimental import pallas as pl
from jax.experimental.pallas import tpu as pltpu
from jax.sharding import PartitionSpec as P

MESH = pl.DeviceIdType.MESH
full_precision = lax.Precision.HIGHEST
eps_norm = 1e-06
shrink_level = 0.01


def layer_norm(values, scaling, offset):
    average = jnp.mean(values, axis=-1, keepdims=True)
    squares = jnp.mean(values * values, axis=-1, keepdims=True)
    variance = squares - average * average
    return (values - average) * lax.rsqrt(variance + eps_norm) * scaling + offset


def soft_shrink(values):
    zeros = jnp.zeros_like(values)
    return jnp.where(
        values > shrink_level,
        values - shrink_level,
        jnp.where(values < -shrink_level, values + shrink_level, zeros),
    )


def split_bf16(array):
    high = array.astype(jnp.bfloat16)
    return high, (array - high.astype(jnp.float32)).astype(jnp.bfloat16)


def host_split(array):
    whole = np.asarray(array, np.float32)
    high = whole.astype(jnp.bfloat16)
    low = (whole - high.astype(np.float32)).astype(jnp.bfloat16)
    return jnp.asarray(np.stack([high, low]))


def transforms(latitudes, longitudes, bands):
    kept = longitudes // 2
    each, rows = kept // bands, latitudes // bands
    waves = np.arange(kept).reshape(bands, each).T.reshape(-1)
    lats = np.arange(latitudes).reshape(bands, rows).T.reshape(-1)
    lon = np.outer(waves, np.arange(longitudes)) % longitudes * (2.0 * math.pi / longitudes)
    lat = np.outer(np.arange(latitudes), lats) % latitudes * (2.0 * math.pi / latitudes)
    forward = np.concatenate([np.cos(lon), -np.sin(lon)], 0) / math.sqrt(longitudes)
    across = np.stack([np.cos(lat), np.sin(lat)], 0) / math.sqrt(latitudes)
    weight = np.where(waves == 0, 1.0, 2.0)[:, None]
    inverse = np.concatenate([np.cos(lon) * weight, -np.sin(lon) * weight], 0).T
    return (
        host_split(forward),
        host_split(across.reshape(2 * latitudes, latitudes)),
        host_split(across.transpose(0, 2, 1).reshape(2 * latitudes, latitudes)),
        host_split(inverse / math.sqrt(longitudes)),
    )


def mix_matrices(weights, biases):
    slot, width = weights.shape[-2:]
    groups = slot // width
    eye = jnp.eye(groups, dtype=weights.dtype)
    full = weights.reshape(2, 2, groups, width, 1, width) * eye[None, None, :, None, :, None]
    full = full.reshape(2, 2, slot, slot)
    whole = jnp.concatenate(
        [
            jnp.concatenate([full[:, 0], full[:, 1]], axis=2),
            jnp.concatenate([-full[:, 1], full[:, 0]], axis=2),
        ],
        axis=1,
    )
    def lanes(array, axis):
        part = [lax.slice_in_dim(array, a, b, axis=axis) for a, b in
                ((0, 128), (slot, slot + 128), (128, slot), (slot + 128, 2 * slot))]
        return jnp.concatenate(part, axis=axis)
    whole = lanes(lanes(whole, 1), 2)
    high, low = split_bf16(whole)
    offsets = lanes(biases.reshape(2, 2 * slot), 1)
    return jnp.stack([high, low], axis=1), jnp.concatenate([offsets, jnp.zeros((6, 2 * slot))], 0)


def product(left, right):
    total = None
    for a, b in ((0, 0), (1, 0), (0, 1)):
        if a < len(left) and b < len(right):
            term = jnp.dot(left[a], right[b], preferred_element_type=jnp.float32)
            total = term if total is None else total + term
    return total


directions = [(b, c) for b in (-1, 0, 1) for c in (-1, 0, 1) if (b, c) != (0, 0)]


def ocean_selectors(quarter):
    columns = np.arange(-8, 2 * quarter + 8)
    pick = np.zeros((len(columns), 384), np.float32)
    seen = np.zeros((len(columns), 512), np.float32)
    for i, column in enumerate(columns):
        if not -3 <= column < 2 * quarter + 3:
            continue
        token = column // 2
        side = 0 if token < 0 else 2 if token >= quarter else 1
        pick[i, side * 128 + token % quarter] = 1
        inner = column % (2 * quarter)
        seen[i, inner - 128 if column < 0 else 384 + inner if column >= 2 * quarter else 128 + inner] = 1
    split = np.zeros((2 * quarter, 2 * quarter), np.float32)
    for e in range(2):
        split[e * quarter + np.arange(quarter), 2 * np.arange(quarter) + e] = 1
    return (jnp.asarray(m, jnp.bfloat16) for m in (pick, seen, split))


def thirds(array):
    high = array.astype(jnp.bfloat16)
    rest = array - high.astype(jnp.float32)
    middle = rest.astype(jnp.bfloat16)
    return high, middle, (rest - middle.astype(jnp.float32)).astype(jnp.bfloat16)


def gelu(z):
    return 0.5 * z * (1.0 + lax.erf(z * math.sqrt(0.5)))


def step_kernel(bands, *refs):
    (
        x_ref, affine_ref, forward_ref, across_ref, back_ref, inverse_ref, mix_ref, offset_ref,
        second_ref, fc_in_ref, fc_out_ref, share_ref, ocean_ref, mask_ref, spread_ref, depth_ref,
        ocean_affine_ref, ocean_in_ref, ocean_out_ref, field_ref, pick_ref, seen_ref, split_ref,
        atmosphere_ref, next_ref, surface_ref,
        normed, after, token, stage, landed, sums, all_sums, send_a, got_a, send_b, got_b,
        w_in, w_out, stream, hidden_ref, half_out, half_in, part_out, part_in, shared_ref,
        rows_in, cols_in, corner_in, masks_in, flux_ref, flux_in, tile_ref, conv_ref, wave_ref,
        middle_out, middle_in,
        sent_sum, came_sum, sent_a, came_a, sent_b, came_b, sent_out, came_out,
        sent_half, came_half, sent_part, came_part, load, sent_load, came_load,
        sent_share, came_share, sent_cells, came_cells, sent_mask, came_mask, sent_flux, came_flux,
        sent_middle, came_middle,
    ) = refs
    rows, longitudes, slot = x_ref.shape
    quarter = longitudes // 4
    middle = quarter // 2
    latitudes = rows * bands
    each = longitudes // 2 // bands
    cells = ocean_ref.shape[1]
    me = lax.axis_index("band")
    comp, tile = lax.axis_index("comp"), lax.axis_index("tile")
    mine = comp * 2 + tile

    def member(step):
        return lax.rem(mine + step, 4)

    def team_id(index):
        return {"comp": lax.div(index, 2), "tile": lax.rem(index, 2)}

    def near_id(b, c):
        index = lax.rem(mine + c + 4, 4)
        return {"band": lax.rem(me + b + bands, bands), **team_id(index)}

    own_loads = [
        pltpu.make_async_copy(source.at[block], target.at[block, 0], load.at[block, i])
        for block in range(2)
        for i, (source, target) in enumerate(((fc_in_ref, w_in), (fc_out_ref, w_out)))
    ]
    sibling_loads = [
        pltpu.make_async_remote_copy(
            src_ref=source.at[block],
            dst_ref=target.at[block, 1],
            send_sem=sent_load.at[block, i],
            recv_sem=came_load.at[block, i],
            device_id={"tile": 1 - tile},
            device_id_type=MESH,
        )
        for block in range(2)
        for i, (source, target) in enumerate(((fc_in_ref, w_in), (fc_out_ref, w_out)))
    ]
    barrier = pltpu.get_barrier_semaphore()

    def greet(step, carry):
        pl.semaphore_signal(
            barrier, inc=1, device_id={"band": lax.rem(me + step, bands)}, device_id_type=MESH
        )
        return carry

    for step in range(1, 4):
        pl.semaphore_signal(barrier, inc=1, device_id=team_id(member(step)), device_id_type=MESH)
    for b, c in directions:
        if b and c:
            pl.semaphore_signal(barrier, inc=1, device_id=near_id(b, c), device_id_type=MESH)
    lax.fori_loop(1, bands, greet, 0)
    for copy in own_loads:
        copy.start()

    def near_copies(source_of, target_of, sent, came):
        copies = []
        for d, (b, c) in enumerate(directions):
            copies.append(
                pltpu.make_async_remote_copy(
                    src_ref=source_of(b, c),
                    dst_ref=target_of(-b, -c),
                    send_sem=sent.at[d],
                    recv_sem=came.at[directions.index((-b, -c))],
                    device_id=near_id(b, c),
                    device_id_type=MESH,
                )
            )
        return copies

    def near_landings(source_of, target_of, sent, came):
        copies = []
        for d, (b, c) in enumerate(directions):
            copies.append(
                pltpu.make_async_remote_copy(
                    src_ref=source_of(b, c),
                    dst_ref=target_of(b, c),
                    send_sem=sent.at[d],
                    recv_sem=came.at[d],
                    device_id=near_id(b, c),
                    device_id_type=MESH,
                )
            )
        return copies

    def cells_from(b, c):
        row = pl.ds(0, 2 * rows) if b == 0 else pl.ds(2 * rows - 3 if b > 0 else 0, 3)
        column = pl.ds(0, cells) if c == 0 else pl.ds(cells - 16 if c > 0 else 0, 16)
        return ocean_ref.at[row, column]

    def cells_to(b, c):
        if c == 0:
            return rows_in.at[0 if b < 0 else 1]
        if b == 0:
            return cols_in.at[0 if c < 0 else 1]
        return corner_in.at[0 if b < 0 else 1, 0 if c < 0 else 1]

    cell_args = (cells_from, cells_to, sent_cells, came_cells)
    mask_args = (
        lambda b, c: mask_ref, lambda b, c: masks_in.at[directions.index((b, c))], sent_mask, came_mask
    )
    flux_args = (
        lambda b, c: flux_ref, lambda b, c: flux_in.at[directions.index((b, c))], sent_flux, came_flux
    )

    def team_copy(source, target, sent, came, step, pick, landing):
        index = member(step)
        chosen = {"whole": lambda: source, "half": lambda: source.at[lax.rem(index, 2)],
                  "each": lambda: source.at[index]}[pick]()
        place = index if landing else mine
        return pltpu.make_async_remote_copy(
            src_ref=chosen,
            dst_ref=target.at[place],
            send_sem=sent.at[index],
            recv_sem=came.at[place],
            device_id=team_id(index),
            device_id_type=MESH,
        )

    def team_exchange(source, target, sent, came, pick):
        for step in range(1, 4):
            team_copy(source, target, sent, came, step, pick, False).start()

    def team_finish(source, target, sent, came, pick):
        for step in range(1, 4):
            team_copy(source, target, sent, came, step, pick, True).wait()

    def band_copy(source, target, sent, came, step, landing):
        index = lax.rem(me + step, bands)
        return pltpu.make_async_remote_copy(
            src_ref=source.at[index],
            dst_ref=target.at[index if landing else me],
            send_sem=sent.at[index],
            recv_sem=came.at[index if landing else me],
            device_id={"band": index},
            device_id_type=MESH,
        )

    def band_exchange(source, target, sent, came):
        source[...] = stage[...].astype(jnp.bfloat16).reshape(source.shape)

        def go(step, carry):
            band_copy(source, target, sent, came, step, False).start()
            return carry

        lax.fori_loop(1, bands, go, 0)
        target[me] = source[me]

        def come(step, carry):
            band_copy(source, target, sent, came, step, True).wait()
            return carry

        lax.fori_loop(1, bands, come, 0)
        landed[...] = target[...].astype(jnp.float32).reshape(landed.shape)

    lane = lax.broadcasted_iota(jnp.int32, (1, 128), 1)
    first_half = lane < slot - 128
    sign = jnp.where(first_half, 1.0, -1.0)
    half = longitudes // 2
    counted = jnp.where(lax.broadcasted_iota(jnp.int32, (8, 256), 1) < slot, 1.0, 0.0)
    counted = counted.astype(jnp.bfloat16)
    which = lax.broadcasted_iota(jnp.int32, (8, longitudes), 0)
    turned = (((1,), (1,)), ((), ()))

    def across_rows(left, right):
        return lax.dot_general(left, right, turned, preferred_element_type=jnp.float32)

    def swap(values):
        return pltpu.roll(values, 64, 1)

    def doubled(tails):
        top = jnp.where(first_half, tails, swap(tails))
        low = jnp.where(first_half, swap(tails), tails)
        return jnp.concatenate([top, low], axis=0)

    def tokens(block, lat):
        if block == 0:
            values = x_ref[lat].astype(jnp.float32)
            return jnp.concatenate([values, values[:, 128:]], axis=1)
        pieces = [middle_in[s, lat].astype(jnp.float32) for s in range(4)]
        return jnp.concatenate(
            [jnp.concatenate([p[:quarter], doubled(p[quarter:])], axis=1) for p in pieces], axis=0
        )

    def spread(lat, wave, part, values):
        stage[pl.ds(part * 9 + lat * 3 + wave, bands, stride=32), :] = values

    def collect(lat, wave, part):
        return landed[pl.ds(part * 9 + lat * 3 + wave, bands, stride=32), :]

    def spectral_filter(block):
        total = jnp.zeros((8, longitudes), jnp.float32)
        for lat in range(rows):
            values = tokens(block, lat)
            high, low = split_bf16(values * values)
            total = total + jnp.where(
                which == lat, across_rows(counted, values.astype(jnp.bfloat16)), 0.0
            )
            total = total + jnp.where(
                which == rows + lat, across_rows(counted, high) + across_rows(counted, low), 0.0
            )
        sums[...] = total
        if block == 0:
            pl.semaphore_wait(barrier, bands - 1 + 3 + 4)
        team_exchange(sums, all_sums.at[block], sent_sum.at[block], came_sum.at[block], "whole")
        if block == 0:
            for copy in near_copies(*mask_args) + near_copies(*cell_args) + sibling_loads:
                copy.start()
            team_exchange(share_ref, shared_ref, sent_share, came_share, "whole")
            shared_ref[mine] = share_ref[...]
        all_sums[block, mine] = total
        team_finish(sums, all_sums.at[block], sent_sum.at[block], came_sum.at[block], "whole")
        total = (
            all_sums[block, 0] + all_sums[block, 1] + all_sums[block, 2] + all_sums[block, 3]
        ) * (1.0 / (4 * slot))
        columns = jnp.concatenate([total, jnp.zeros((120, longitudes), jnp.float32)], axis=0).T
        for lat in range(rows):
            average = columns[:, lat : lat + 1]
            power = columns[:, rows + lat : rows + lat + 1]
            scaled = tokens(block, lat) - average
            scaled = scaled * lax.rsqrt(power - average * average + eps_norm)
            scaled = scaled * affine_ref[block, 0:1, :] + affine_ref[block, 1:2, :]
            normed[lat] = scaled
            spectrum = product((forward_ref[0], forward_ref[1]), split_bf16(scaled))
            upper, lower = spectrum[:half], spectrum[half:]
            rest = jnp.where(first_half, upper[:, 128:], lower[:, 128:])
            parts = (upper[:, :128], lower[:, :128], rest)
            for part in range(3):
                for wave in range(each):
                    spread(lat, wave, part, parts[part][wave * bands : (wave + 1) * bands])
        band_exchange(send_a, got_a.at[block], sent_a.at[block], came_a.at[block])
        pieces = []
        for wave in range(each):
            for part in range(3):
                pieces.append(
                    jnp.concatenate([collect(lat, wave, part) for lat in range(rows)], axis=0)
                )
        spectrum = jnp.concatenate(pieces, axis=1).astype(jnp.bfloat16)
        turned_all = product((across_ref[0], across_ref[1]), (spectrum,))

        def combine(both, wave, direction):
            base = wave * 384
            cosine, sine = both[:latitudes, base : base + 384], both[latitudes:, base : base + 384]
            real = cosine[:, :128] + direction * sine[:, 128:256]
            imag = cosine[:, 128:256] - direction * sine[:, :128]
            rest = cosine[:, 256:] + (direction * sign) * swap(sine[:, 256:])
            return real, imag, rest

        rows_mixed = jnp.concatenate(
            [jnp.concatenate(combine(turned_all, wave, 1.0), axis=1) for wave in range(each)], axis=0
        )
        hidden = product(split_bf16(rows_mixed), (mix_ref[block, 0, 0], mix_ref[block, 0, 1]))
        hidden = jnp.maximum(hidden + offset_ref[block, 0:1, :], 0.0)
        mixed = product(split_bf16(hidden), (mix_ref[block, 1, 0], mix_ref[block, 1, 1]))
        mixed = soft_shrink(mixed + offset_ref[block, 1:2, :])
        mixed = jnp.concatenate(
            [mixed[wave * latitudes : (wave + 1) * latitudes] for wave in range(each)], axis=1
        )
        turned_back = product((back_ref[0], back_ref[1]), split_bf16(mixed))
        for wave in range(each):
            parts = combine(turned_back, wave, -1.0)
            for part in range(3):
                for lat in range(rows):
                    spread(lat, wave, part, parts[part][lat * bands : (lat + 1) * bands])
        band_exchange(send_b, got_b.at[block], sent_b.at[block], came_b.at[block])
        for lat in range(rows):
            real, imag, rest = (
                jnp.concatenate([collect(lat, wave, part) for wave in range(each)], axis=0)
                for part in range(3)
            )
            right = jnp.concatenate(
                [
                    jnp.concatenate([real, rest], axis=1),
                    jnp.concatenate([imag, swap(rest)], axis=1),
                ],
                axis=0,
            ).astype(jnp.bfloat16)
            restored = product((inverse_ref[0], inverse_ref[1]), (right,))
            result = tokens(block, lat) + restored + normed[lat]
            for s in range(4):
                piece = result[s * quarter : (s + 1) * quarter]
                tail = piece[:, 128:]
                tail = jnp.where(first_half, tail[:middle], swap(tail[middle:]))
                after[s % 2, s // 2, lat, :quarter] = piece[:, :128].astype(jnp.bfloat16)
                after[s % 2, s // 2, lat, quarter:] = tail.astype(jnp.bfloat16)
        args = (after, token.at[block], sent_out.at[block], came_out.at[block], "half")
        team_exchange(*args)
        token[block, mine] = after[tile]
        team_finish(*args)
        for i in range(2):
            own_loads[2 * block + i].wait()
            sibling_loads[2 * block + i].wait()

    def pair(left, right):
        return jnp.concatenate(
            [jnp.where(first_half, left, swap(right)), jnp.where(first_half, swap(left), right)], 0
        )

    def unpair(both):
        top, low = both[:middle], both[middle:]
        return jnp.where(first_half, top, swap(low)), jnp.where(first_half, swap(top), low)

    def pack(block_rows, target):
        tails = unpair(block_rows[:, 512:640]) + unpair(block_rows[:, 640:])
        for s in range(4):
            place = target(s)
            place[:quarter] = block_rows[:, s * 128 : (s + 1) * 128].astype(jnp.bfloat16)
            place[quarter:] = tails[s].astype(jnp.bfloat16)

    def lanes_of(slices):
        heads = [p[:quarter] for p in slices]
        tails = [p[quarter:] for p in slices]
        return jnp.concatenate(heads + [pair(*tails[:2]), pair(*tails[2:])], axis=1)

    def reorder(values):
        t = [values[:, i * 128 : (i + 1) * 128] for i in range(6)]

        def inner(a, b):
            return jnp.where(first_half, swap(a), swap(b)), jnp.where(first_half, a, b)

        one, tails_a = inner(t[1], t[2])
        three, tails_b = inner(t[4], t[5])
        return jnp.concatenate([t[0], one, t[3], three, tails_a, tails_b], axis=1)

    row_spans = [(s * slot, 128) for s in range(4)] + [(s * slot + 128, slot - 128) for s in range(4)]

    def mlp(block, which_quarter):
        for lat in range(rows):
            slices = [token[block, s, which_quarter, lat].astype(jnp.float32) for s in range(4)]
            stream[lat * quarter : (lat + 1) * quarter] = lanes_of(slices)
        values = stream[...]
        normal = layer_norm(values, second_ref[block, 0:1, :], second_ref[block, 1:2, :])
        normal = normal.astype(jnp.bfloat16)
        wide = w_in.shape[3]
        for part in range(2):

            def piece(i, carry):
                at = pl.multiple_of(i * 256, 256)
                weight = jnp.concatenate(
                    [w_in[block, part, pl.ds(a, n), pl.ds(at, 256)] for a, n in row_spans], axis=0
                )
                z = jnp.dot(normal, weight, preferred_element_type=jnp.float32)
                hidden_ref[:, pl.ds(part * wide + at, 256)] = gelu(z).astype(jnp.bfloat16)
                return carry

            lax.fori_loop(0, wide // 256, piece, 0)
        total = jnp.dot(hidden_ref[:, :wide], w_out[block, 0], preferred_element_type=jnp.float32)
        total = total + jnp.dot(
            hidden_ref[:, wide:], w_out[block, 1], preferred_element_type=jnp.float32
        )
        return reorder(total)

    spectral_filter(0)
    team_finish(share_ref, shared_ref, sent_share, came_share, "whole")
    half_out[...] = mlp(0, 1 - comp).astype(jnp.bfloat16)
    copy = pltpu.make_async_remote_copy(
        src_ref=half_out,
        dst_ref=half_in,
        send_sem=sent_half.at[0],
        recv_sem=came_half.at[0],
        device_id={"comp": 1 - comp},
        device_id_type=MESH,
    )
    copy.start()
    total = mlp(0, comp)
    copy.wait()
    first = stream[...] + total + half_in[...].astype(jnp.float32)
    first = first.astype(jnp.bfloat16)
    stream[...] = first.astype(jnp.float32)

    small = [shared_ref[s] for s in range(4)]
    tails = [s[:, 128:] for s in small]
    whole = jnp.concatenate(
        [s[:, :128] for s in small]
        + [jnp.where(first_half, tails[i], swap(tails[i + 1])) for i in (0, 2)],
        axis=1,
    )
    head, embed = whole[:8].astype(jnp.bfloat16), whole[8:]
    for lat in range(rows):
        flux = across_rows(head, first[lat * quarter : (lat + 1) * quarter])
        flux_ref[lat] = jnp.concatenate([flux, jnp.zeros((8, 128 - quarter), jnp.float32)], axis=1)
    for copy in near_copies(*flux_args):
        copy.start()
    for copy in near_landings(*mask_args) + near_landings(*cell_args) + near_landings(*flux_args):
        copy.wait()

    def flux_at(lat, c):
        b = -1 if lat < 0 else 1 if lat >= rows else 0
        if (b, c) == (0, 0):
            return flux_ref[lat]
        return flux_in[directions.index((b, c)), lat % rows]

    ext_lats = range(-2, rows + 2)
    laid = jnp.concatenate(
        [jnp.concatenate([flux_at(lat, c) for c in (-1, 0, 1)], axis=1) for lat in ext_lats]
        + [jnp.zeros((128 - 8 * len(ext_lats), 384), jnp.float32)],
        axis=0,
    )
    raised = across_rows(pick_ref[...], jnp.concatenate(thirds(laid), axis=0))
    raised = raised[:, :128] + raised[:, 128:256] + raised[:, 256:]
    forcing = product(split_bf16(raised), (spread_ref[0], spread_ref[1]))

    def mask_rows(b, c):
        whole = mask_ref[...] if (b, c) == (0, 0) else masks_in[directions.index((b, c))]
        whole = whole[:, 128:] if c < 0 else whole[:, :128] if c > 0 else whole
        return whole[2 * rows - 3 : 2 * rows] if b < 0 else whole[:3] if b > 0 else whole[: 2 * rows]

    ext_rows = 2 * rows + 6
    masks = jnp.concatenate(
        [jnp.concatenate([mask_rows(b, c) for c in (-1, 0, 1)], axis=1) for b in (-1, 0, 1)]
        + [jnp.zeros((16 - ext_rows, 512), jnp.float32)],
        axis=0,
    )
    masks = across_rows(seen_ref[...], masks.astype(jnp.bfloat16))
    for row in range(ext_rows):
        b = -1 if row < 3 else 1 if row >= 2 * rows + 3 else 0
        at = row if b < 0 else row - 3 if b == 0 else row - 2 * rows - 3
        sources = (
            cols_in[0, at] if b == 0 else corner_in[0 if b < 0 else 1, 0, at],
            ocean_ref[at] if b == 0 else rows_in[0 if b < 0 else 1, at],
            cols_in[1, at] if b == 0 else corner_in[0 if b < 0 else 1, 1, at],
        )
        sources = [s.astype(jnp.float32) for s in sources]
        state = jnp.concatenate([sources[0][8:], sources[1], sources[2][:8]], axis=0)
        level = (row - 3) // 2 + 2
        start = state + masks[:, row : row + 1] * forcing[:, level * 256 : (level + 1) * 256]
        start = start.astype(jnp.bfloat16).astype(jnp.float32)
        if b:
            inside = jnp.where(me > 0, 1.0, 0.0) if b < 0 else jnp.where(me < bands - 1, 1.0, 0.0)
            start = start * inside
        for part in range(2):
            tile_ref[part, row] = start[:, part * 128 : (part + 1) * 128]

    for part in range(2):
        span = slice(part * 128, (part + 1) * 128)

        def strip(i, carry):
            at = pl.multiple_of(i * 16, 16)
            totals = [jnp.zeros((16, 128), jnp.float32) for _ in range(2 * rows)]
            for e in range(7):
                for row in range(ext_rows):
                    values = tile_ref[part, row, pl.ds(at + 5 + e, 16), :]
                    for a in range(7):
                        if 0 <= row - a < 2 * rows:
                            tap = depth_ref[a * 7 + e : a * 7 + e + 1, span]
                            totals[row - a] = totals[row - a] + values * tap
            for row in range(2 * rows):
                conv_ref[row, pl.ds(at, 16), span] = totals[row]
            return carry

        lax.fori_loop(0, cells // 16, strip, 0)

    own_columns = jnp.concatenate([mask_ref[...], jnp.zeros((120, 256), jnp.float32)], axis=0).T
    for start_row in range(0, 2 * rows, 2):
        values = conv_ref[start_row : start_row + 2].reshape(2 * cells, 256)
        normal = layer_norm(values, ocean_affine_ref[0:1, :], ocean_affine_ref[1:2, :])
        normal = normal.astype(jnp.bfloat16)

        def piece(i, carry):
            at = pl.multiple_of(i * 256, 256)
            z = jnp.dot(normal, ocean_in_ref[:, pl.ds(at, 256)], preferred_element_type=jnp.float32)
            wave_ref[:, pl.ds(at, 256)] = gelu(z).astype(jnp.bfloat16)
            return carry

        lax.fori_loop(0, ocean_in_ref.shape[1] // 256, piece, 0)
        update = jnp.dot(wave_ref[...], ocean_out_ref[...], preferred_element_type=jnp.float32)
        update = update * ocean_affine_ref[2:3, :]
        for row in range(start_row, start_row + 2):
            begin = jnp.concatenate([tile_ref[part, row + 3, 8 : 8 + cells] for part in range(2)], axis=1)
            change = update[(row - start_row) * cells : (row - start_row + 1) * cells]
            fresh = (begin + own_columns[:cells, row : row + 1] * change).astype(jnp.bfloat16)
            next_ref[row] = fresh
            field = across_rows(field_ref[...], fresh)
            field = (field[:8] + field[8:16] + field[16:24]) * mask_ref[row : row + 1, :cells]
            surface_ref[row] = field

    for lat in range(rows):
        both = jnp.concatenate([surface_ref[2 * lat], surface_ref[2 * lat + 1]], axis=0)
        patch = across_rows(split_ref[...], jnp.concatenate(thirds(both), axis=0))
        patch = patch[:, :16] + patch[:, 16:32] + patch[:, 32:48]
        total = stream[lat * quarter : (lat + 1) * quarter]
        for e in range(2):
            total = total + product(
                split_bf16(patch[e * quarter : (e + 1) * quarter]),
                split_bf16(embed[e * 16 : (e + 1) * 16]),
            )
        pack(total, lambda s, lat=lat: middle_out.at[s, lat])
    args = (middle_out, middle_in, sent_middle, came_middle, "each")
    team_exchange(*args)
    middle_in[mine] = middle_out[mine]
    team_finish(*args)

    spectral_filter(1)
    for which_quarter in range(2):
        total = mlp(1, which_quarter)
        for lat in range(rows):
            pack(
                total[lat * quarter : (lat + 1) * quarter],
                lambda s, lat=lat: part_out.at[which_quarter, s, lat],
            )
        team_exchange(
            part_out.at[which_quarter], part_in.at[which_quarter],
            sent_part.at[which_quarter], came_part.at[which_quarter], "each",
        )
        part_in[which_quarter, mine] = part_out[which_quarter, mine]
    for which_quarter in range(2):
        team_finish(
            part_out.at[which_quarter], part_in.at[which_quarter],
            sent_part.at[which_quarter], came_part.at[which_quarter], "each",
        )
        for half_of in range(2):
            for lat in range(rows):
                piece = after[half_of, which_quarter, lat].astype(jnp.float32)
                piece = piece + part_in[which_quarter, half_of, lat].astype(jnp.float32)
                piece = piece + part_in[which_quarter, 2 + half_of, lat].astype(jnp.float32)
                tail = piece[quarter:]
                at = (2 * which_quarter + half_of) * quarter
                tail = jnp.concatenate([tail, swap(tail)], axis=0)
                atmosphere_ref[lat, at : at + quarter, :128] = piece[:quarter].astype(jnp.bfloat16)
                atmosphere_ref[lat, at : at + quarter, 128:] = tail[:, : slot - 128].astype(
                    jnp.bfloat16
                )


def on_device(
    atmosphere, spec_weight, spec_bias, norm_gain, norm_shift, fc_in, fc_out, flux_head, flux_embed,
    ocean_state, sea_mask, depth_kernel, ocean_gain, ocean_shift, ocean_in, ocean_out, layer_scale,
    field_head, patch_embed,
):
    column_index = lax.axis_index(("comp", "tile"))
    bands = lax.axis_size("band")
    rows, longitudes, slot = atmosphere.shape
    quarter = longitudes // 4
    count = rows * quarter
    latitudes = rows * bands
    channels, wide = fc_in.shape[1:]
    packed = quarter * slot // 128
    cells, ocean_channels = ocean_state.shape[1:]
    waves = ocean_in.shape[1]

    def heads_first(array):
        split = array.reshape(array.shape[:-1] + (4, slot))
        lead = array.shape[:-1]
        return jnp.concatenate(
            [split[..., :128].reshape(lead + (-1,)), split[..., 128:].reshape(lead + (-1,))], axis=-1
        )

    def taller(array, height):
        return jnp.pad(array, ((0, 0),) * (array.ndim - 2) + ((0, height - array.shape[-2]), (0, 0)))

    affine = jnp.stack([norm_gain[:, 0], norm_shift[:, 0]], axis=1)
    affine = lax.dynamic_slice_in_dim(affine, column_index * slot, slot, axis=2)
    affine = taller(jnp.concatenate([affine, affine[:, :, 128:]], axis=2), 8)
    second = taller(heads_first(jnp.stack([norm_gain[:, 1], norm_shift[:, 1]], axis=1)), 8)
    mixes = [mix_matrices(spec_weight[b], spec_bias[b]) for b in range(2)]
    mix = jnp.stack([m[0] for m in mixes])
    offsets = jnp.stack([m[1] for m in mixes])
    patch = patch_embed.reshape(4, 2, 2, slot).transpose(2, 1, 0, 3)
    patch = jnp.pad(patch, ((0, 0), (0, 0), (0, 4), (0, 0))).reshape(32, slot)
    share = jnp.concatenate([flux_head.astype(jnp.float32).T, patch], axis=0)
    share = jnp.pad(share, ((0, 0), (0, 256 - slot)))
    mask = jnp.pad(sea_mask.astype(jnp.float32), ((0, 8 - sea_mask.shape[0]), (0, 256 - cells)))
    levels = rows + 4
    embed = jnp.eye(levels)[:, None, :, None] * flux_embed[None, :, None, :]
    embed = taller(embed.reshape(levels * 8, levels * ocean_channels), 128)
    embed = jnp.stack(split_bf16(embed))
    depth = taller(depth_kernel.reshape(49, ocean_channels), 56)
    ocean_affine = taller(jnp.stack([ocean_gain, ocean_shift, layer_scale]), 8)
    field = jnp.concatenate([jnp.pad(f, ((0, 4), (0, 0))) for f in thirds(field_head.T)], axis=0)
    inside, outside = pl.BlockSpec(memory_space=pltpu.VMEM), pl.BlockSpec(memory_space=pl.ANY)
    arguments = [
        atmosphere, affine, *transforms(latitudes, longitudes, bands), mix, offsets, second,
        fc_in, fc_out, share, ocean_state, mask, embed, depth, ocean_affine, ocean_in, ocean_out,
        field, *ocean_selectors(quarter),
    ]
    specs = [inside] * 9 + [outside] * 2 + [inside] * (len(arguments) - 11)
    narrow, single = jnp.bfloat16, jnp.float32

    def dma(*shape):
        return pltpu.SemaphoreType.DMA(shape)

    chunks = (bands, 32, 128)
    scratch = [
        pltpu.VMEM((rows, longitudes, 256), single),
        pltpu.VMEM((2, 2, rows, packed, 128), narrow),
        pltpu.VMEM((2, 4, 2, rows, packed, 128), narrow),
        pltpu.VMEM((bands * 32, 128), single),
        pltpu.VMEM((bands * 32, 128), single),
        pltpu.VMEM((8, longitudes), single),
        pltpu.VMEM((2, 4, 8, longitudes), single),
        pltpu.VMEM(chunks, narrow),
        pltpu.VMEM((2,) + chunks, narrow),
        pltpu.VMEM(chunks, narrow),
        pltpu.VMEM((2,) + chunks, narrow),
        pltpu.VMEM((2, 2, channels, wide), narrow),
        pltpu.VMEM((2, 2, wide, channels), narrow),
        pltpu.VMEM((count, channels), single),
        pltpu.VMEM((count, 2 * wide), narrow),
        pltpu.VMEM((count, channels), narrow),
        pltpu.VMEM((count, channels), narrow),
        pltpu.VMEM((2, 4, rows, packed, 128), narrow),
        pltpu.VMEM((2, 4, rows, packed, 128), narrow),
        pltpu.VMEM((4,) + share.shape, single),
        pltpu.VMEM((2, 3, cells, ocean_channels), narrow),
        pltpu.VMEM((2, 2 * rows, 16, ocean_channels), narrow),
        pltpu.VMEM((2, 2, 3, 16, ocean_channels), narrow),
        pltpu.VMEM((8,) + mask.shape, single),
        pltpu.VMEM((rows, 8, 128), single),
        pltpu.VMEM((8, rows, 8, 128), single),
        pltpu.VMEM((2, 2 * rows + 6, cells + 16, 128), single),
        pltpu.VMEM((2 * rows, cells, ocean_channels), single),
        pltpu.VMEM((2 * cells, waves), narrow),
        pltpu.VMEM((4, rows, packed, 128), narrow),
        pltpu.VMEM((4, rows, packed, 128), narrow),
        dma(2, 4), dma(2, 4), dma(2, bands), dma(2, bands), dma(2, bands), dma(2, bands),
        dma(2, 4), dma(2, 4), dma(1), dma(1), dma(2, 4), dma(2, 4), dma(2, 2), dma(2, 2), dma(2, 2),
        dma(4), dma(4), dma(8), dma(8), dma(8), dma(8), dma(8), dma(8), dma(4), dma(4),
    ]
    atmosphere_next, ocean_next, surface = pl.pallas_call(
        functools.partial(step_kernel, bands),
        out_shape=(
            jax.ShapeDtypeStruct(atmosphere.shape, narrow),
            jax.ShapeDtypeStruct(ocean_state.shape, narrow),
            jax.ShapeDtypeStruct((2 * rows, 8, cells), single),
        ),
        in_specs=specs,
        out_specs=(inside,) * 3,
        scratch_shapes=scratch,
        compiler_params=pltpu.CompilerParams(
            collective_id=0, has_side_effects=True, vmem_limit_bytes=63 << 20
        ),
    )(*arguments)
    return (atmosphere_next, ocean_next, surface[:, :4].transpose(0, 2, 1))


def solution(mesh):
    placed = (
        P("band", None, ("comp", "tile")),
        P(None, None, None, ("comp", "tile"), None),
        P(None, None, None, ("comp", "tile")),
        P(),
        P(),
        P(None, None, ("comp", "tile")),
        P(None, ("comp", "tile"), None),
        P(("comp", "tile"), None),
        P(),
        P("band", ("comp", "tile"), None),
        P("band", ("comp", "tile")),
        P(),
        P(),
        P(),
        P(),
        P(),
        P(),
        P(),
        P(None, ("comp", "tile")),
    )
    return jax.shard_map(
        on_device,
        mesh=mesh,
        in_specs=placed,
        out_specs=(
            P("band", None, ("comp", "tile")),
            P("band", ("comp", "tile"), None),
            P("band", ("comp", "tile"), None),
        ),
        check_vma=False,
    )
```

time: 316 us -> 210 us (0.66); the launches traced: 311 us -> 209 us
  matrix products: 42.6 us -> 0 us
  blocking collectives: 29.7 us -> 0 us
  Pallas kernels: 162 us -> 189 us
  local copies, waits for them, and re-layouts: 26.3 us -> 11.3 us
  between operations: 15.4 us -> 0.96 us
  other arithmetic: 21 us -> 8.41 us
  waiting for transfers between devices: 8.37 us -> 0 us
  starting transfers between devices: 5.72 us -> 0 us
    dot_general x7 -> x0, matrix products: 42.6 us -> none  [the longest x2 27.8 us: channel_mlp(): summed = jnp.dot(hidden, w_out, preferred_element_type=jnp.float32)]
    pallas_call x2 -> x1, Pallas kernels: 162 us -> 189 us  [on_device(): pl.pallas_call(functools.partial(step_kernel, bands), out_shape=(jax.Shap...]
    all_to_all x1 -> x0, blocking collectives: 15 us -> none  [on_device(): lax.all_to_all(result, team, split_axis=2, concat_axis=1, tiled=True)]
    all_gather x2 -> x0, blocking collectives: 14.7 us -> none  [the longest x1 8.72 us: on_device(): embed = lax.all_gather(patch_embed, team, axis=1, tiled=True)]
    reduce_sum x3 -> x0, other arithmetic: 11.8 us -> none  [layer_norm(): average = jnp.mean(values, axis=-1, keepdims=True)]
    slice x11 -> x6, local copies, waits for them, and re-layouts: 8.67 us -> 1.2 us  [the longest x2 1.17 us: on_device(): mixes = [mix_matrices(spec_weight[b], spec_bias[b]) for b in range(2)]]
    ppermute x4 -> x0, waiting for transfers between devices: 7.1 us -> none  [the longest x2 3.96 us: with_halo(): lax.ppermute(head, axis, [((i + 1) % count, i) for i in range(ends)])]
    ppermute x4 -> x0, starting transfers between devices: 5.56 us -> none  [the longest x2 4.27 us: with_halo(): lax.ppermute(tail, axis, [(i, (i + 1) % count) for i in range(ends)])]
  transfers between devices with their start and end apart: 8 -> 0, of which waited for: 2 -> 0; matrix products, arithmetic and copies ran while one was open for 22% -> 0% of each run, Pallas kernels for 52% -> 0%
where the time goes in v1:
time: 210 us; the launch traced here: 209 us
  Pallas kernels  189 us (90%)
  local copies, waits for them, and re-layouts  11.3 us (5%)
  other arithmetic  8.41 us (4%)
    pallas_call x1, Pallas kernels, on_device(): pl.pallas_call(functools.partial(step_kernel, bands), out_shape=(jax.Shap...  189 us

profile of v1, /device:TPU:1, one launch (start us, length us, event | category | flops | bytes accessed | tf_op | source)
XLA Modules:
  0.0 209.4 jit_solution(11945118402787918083)
XLA Ops:
  0.6 1.2 fusion.27
  1.8 0.3 mul.70
  2.1 0.5 mul.71
  2.6 0.3 mul.77
  2.9 0.5 mul.78
  4.0 0.2 fusion.13
  4.8 0.2 subtract_convert_fusion.1
  5.0 0.2 fusion.11
  5.9 0.2 subtract_convert_fusion
  6.2 1.7 pad_maximum_fusion.refs_6_
  8.5 0.6 pad_maximum_fusion.4.refs_7_
  9.2 0.7 select_maximum_fusion.6.refs_1_
  10.1 0.6 select_maximum_fusion.4.refs_8_
  11.0 1.0 pad_maximum_fusion.3.refs_14_
  12.1 0.6 fusion.19.refs_19_
  12.7 1.1 copy.36.refs_0_
  13.7 0.6 pad.50.refs_15_
  14.4 0.6 select_maximum_fusion.5.refs_11_
  15.1 0.6 pad.48.refs_13_
  15.7 0.6 select_maximum_fusion.13.refs_16_
  16.3 188.7 %shard_map.265 = (bf16[3,384,192]{2,1,0:T(8,128)(2,1)}, bf16[6,192,256]{2,1,0:T(8,128)(2,1)}, f32[6,8,192]{2,1,0:T(8,128)}) custom-call(bf16[3,384,192]{2,1,0:T(8,128)(2,1)} %copy.36.refs_0_, f32[2,8,256]{2,1,0:T(8,128)} %select_maximum_fusion.6.refs_1_, bf16[2,384,384]{2,1,0:T(8,128)(2,1)} %constant.33.clone.refs_2_, ...), custom_call_target="tpu_custom_call" | custom-call | tf_op jit(solution)/shard_map/pallas_call | solution.py:761
  205.0 2.1 %copy.37 = bf16[3,384,192]{1,2,0:T(8,128)(2,1)} copy(bf16[3,384,192]{2,1,0:T(8,128)(2,1)} %get-tuple-element.9) | data formatting | bytes 884736
  207.1 1.4 slice_bitcast_fusion.12
  208.5 0.8 copy.43
  (74 shorter events, 3.2 us)
Async XLA Ops:
  6.2 1.7 copy-start.8
  6.2 2.9 %copy-start.5 = (f32[2,2,768]{2,1,0:T(2,128)S(1)}, f32[2,2,768]{2,1,0:T(2,128)}, u32[]{:S(2)}) copy-start(f32[2,2,768]{2,1,0:T(2,128)} %param.29) | copy-start | bytes 36868
  6.2 2.9 %copy-start.6 = (f32[2,2,768]{2,1,0:T(2,128)S(1)}, f32[2,2,768]{2,1,0:T(2,128)}, u32[]{:S(2)}) copy-start(f32[2,2,768]{2,1,0:T(2,128)} %param.30) | copy-start | bytes 36868
  6.2 4.5 %copy-start.7 = (f32[8,256]{1,0:T(8,128)S(1)}, f32[8,256]{1,0:T(8,128)}, u32[]{:S(2)}) copy-start(f32[8,256]{1,0:T(8,128)} %param.34) | copy-start | bytes 24580
  10.9 1.1 copy-start.4
  10.9 1.8 copy-start.1
  11.0 2.8 %copy-start.2 = (f32[7,7,256]{2,1,0:T(8,128)S(1)}, f32[7,7,256]{2,1,0:T(8,128)}, u32[]{:S(2)}) copy-start(f32[7,7,256]{2,1,0:T(8,128)} %param.37) | copy-start | bytes 150532
  11.0 3.4 %copy-start.3 = (f32[16,192]{1,0:T(8,128)S(1)}, f32[16,192]{1,0:T(8,128)}, u32[]{:S(2)}) copy-start(f32[16,192]{1,0:T(8,128)} %param.44) | copy-start | bytes 36868
  11.0 3.4 %copy-start.10 = (bf16[192,8]{0,1:T(8,128)(2,1)S(1)}, bf16[192,8]{0,1:T(8,128)(2,1)}, u32[]{:S(2)}) copy-start(bf16[192,8]{0,1:T(8,128)(2,1)} %param.33) | copy-start | bytes 9220
  12.0 3.0 %copy-start.9 = (s32[6,192]{1,0:T(8,128)S(1)}, s32[6,192]{1,0:T(8,128)}, u32[]{:S(2)}) copy-start(s32[6,192]{1,0:T(8,128)} %param.36) | copy-start | bytes 13828
  12.0 3.7 %copy-start.11 = (f32[256]{0:T(256)S(1)}, f32[256]{0:T(256)}, u32[]{:S(2)}) copy-start(f32[256]{0:T(256)} %param.42) | copy-start | bytes 3076
  12.0 3.7 %copy-start.12 = (f32[256]{0:T(256)S(1)}, f32[256]{0:T(256)}, u32[]{:S(2)}) copy-start(f32[256]{0:T(256)} %param.39) | copy-start | bytes 3076
  12.0 3.7 %copy-start.13 = (f32[256]{0:T(256)S(1)}, f32[256]{0:T(256)}, u32[]{:S(2)}) copy-start(f32[256]{0:T(256)} %param.38) | copy-start | bytes 3076
  205.0 3.5 %copy-start = (bf16[6,192,256]{2,1,0:T(8,128)(2,1)S(1)}, bf16[6,192,256]{2,1,0:T(8,128)(2,1)}, u32[]{:S(2)}) copy-start(bf16[6,192,256]{2,1,0:T(8,128)(2,1)} %get-tuple-element.60) | copy-start | bytes 1769476

commit v2 on v1

--- a/solution.py
+++ b/solution.py
@@ -34,13 +34,6 @@
 def split_bf16(array):
     high = array.astype(jnp.bfloat16)
     return high, (array - high.astype(jnp.float32)).astype(jnp.bfloat16)
-
-
-def host_split(array):
-    whole = np.asarray(array, np.float32)
-    high = whole.astype(jnp.bfloat16)
-    low = (whole - high.astype(np.float32)).astype(jnp.bfloat16)
-    return jnp.asarray(np.stack([high, low]))
 
 
 def transforms(latitudes, longitudes, bands):
@@ -54,35 +47,19 @@
     across = np.stack([np.cos(lat), np.sin(lat)], 0) / math.sqrt(latitudes)
     weight = np.where(waves == 0, 1.0, 2.0)[:, None]
     inverse = np.concatenate([np.cos(lon) * weight, -np.sin(lon) * weight], 0).T
-    return (
-        host_split(forward),
-        host_split(across.reshape(2 * latitudes, latitudes)),
-        host_split(across.transpose(0, 2, 1).reshape(2 * latitudes, latitudes)),
-        host_split(inverse / math.sqrt(longitudes)),
-    )
-
-
-def mix_matrices(weights, biases):
-    slot, width = weights.shape[-2:]
-    groups = slot // width
-    eye = jnp.eye(groups, dtype=weights.dtype)
-    full = weights.reshape(2, 2, groups, width, 1, width) * eye[None, None, :, None, :, None]
-    full = full.reshape(2, 2, slot, slot)
-    whole = jnp.concatenate(
-        [
-            jnp.concatenate([full[:, 0], full[:, 1]], axis=2),
-            jnp.concatenate([-full[:, 1], full[:, 0]], axis=2),
-        ],
-        axis=1,
-    )
-    def lanes(array, axis):
-        part = [lax.slice_in_dim(array, a, b, axis=axis) for a, b in
-                ((0, 128), (slot, slot + 128), (128, slot), (slot + 128, 2 * slot))]
-        return jnp.concatenate(part, axis=axis)
-    whole = lanes(lanes(whole, 1), 2)
-    high, low = split_bf16(whole)
-    offsets = lanes(biases.reshape(2, 2 * slot), 1)
-    return jnp.stack([high, low], axis=1), jnp.concatenate([offsets, jnp.zeros((6, 2 * slot))], 0)
+    mats = (
+        forward,
+        across.reshape(2 * latitudes, latitudes),
+        across.transpose(0, 2, 1).reshape(2 * latitudes, latitudes),
+        inverse / math.sqrt(longitudes),
+    )
+    return [jnp.asarray(m, jnp.bfloat16) for m in mats]
+
+
+def times(left, right):
+    return jnp.dot(
+        left.astype(jnp.bfloat16), right.astype(jnp.bfloat16), preferred_element_type=jnp.float32
+    )
 
 
 def product(left, right):
@@ -128,14 +105,16 @@
 
 def step_kernel(bands, *refs):
     (
-        x_ref, affine_ref, forward_ref, across_ref, back_ref, inverse_ref, mix_ref, offset_ref,
-        second_ref, fc_in_ref, fc_out_ref, share_ref, ocean_ref, mask_ref, spread_ref, depth_ref,
-        ocean_affine_ref, ocean_in_ref, ocean_out_ref, field_ref, pick_ref, seen_ref, split_ref,
+        x_ref, weight_ref, bias_ref, gain_ref, shift_ref, fc_in_ref, fc_out_ref, flux_head_ref,
+        flux_embed_ref, ocean_ref, sea_ref, depth_ref, ocean_gain_ref, ocean_shift_ref,
+        ocean_in_ref, ocean_out_ref, layer_ref, field_head_ref, patch_ref,
+        forward_ref, across_ref, back_ref, inverse_ref, pick_ref, seen_ref, split_ref,
         atmosphere_ref, next_ref, surface_ref,
         normed, after, token, stage, landed, sums, all_sums, send_a, got_a, send_b, got_b,
         w_in, w_out, stream, hidden_ref, half_out, half_in, part_out, part_in, shared_ref,
         rows_in, cols_in, corner_in, masks_in, flux_ref, flux_in, tile_ref, conv_ref, wave_ref,
-        middle_out, middle_in,
+        middle_out, middle_in, order_ref, affine_ref, mix_ref, offset_ref, share_ref, mask_ref,
+        level_ref, spread_ref, field_ref, total_ref,
         sent_sum, came_sum, sent_a, came_a, sent_b, came_b, sent_out, came_out,
         sent_half, came_half, sent_part, came_part, load, sent_load, came_load,
         sent_share, came_share, sent_cells, came_cells, sent_mask, came_mask, sent_flux, came_flux,
@@ -361,9 +340,9 @@
             power = columns[:, rows + lat : rows + lat + 1]
             scaled = tokens(block, lat) - average
             scaled = scaled * lax.rsqrt(power - average * average + eps_norm)
-            scaled = scaled * affine_ref[block, 0:1, :] + affine_ref[block, 1:2, :]
+            scaled = scaled * affine_ref[block, 0:1, :] + affine_ref[block, 2:3, :]
             normed[lat] = scaled
-            spectrum = product((forward_ref[0], forward_ref[1]), split_bf16(scaled))
+            spectrum = times(forward_ref[...], scaled)
             upper, lower = spectrum[:half], spectrum[half:]
             rest = jnp.where(first_half, upper[:, 128:], lower[:, 128:])
             parts = (upper[:, :128], lower[:, :128], rest)
@@ -378,7 +357,7 @@
                     jnp.concatenate([collect(lat, wave, part) for lat in range(rows)], axis=0)
                 )
         spectrum = jnp.concatenate(pieces, axis=1).astype(jnp.bfloat16)
-        turned_all = product((across_ref[0], across_ref[1]), (spectrum,))
+        turned_all = times(across_ref[...], spectrum)
 
         def combine(both, wave, direction):
             base = wave * 384
@@ -391,14 +370,14 @@
         rows_mixed = jnp.concatenate(
             [jnp.concatenate(combine(turned_all, wave, 1.0), axis=1) for wave in range(each)], axis=0
         )
-        hidden = product(split_bf16(rows_mixed), (mix_ref[block, 0, 0], mix_ref[block, 0, 1]))
+        hidden = times(rows_mixed, mix_ref[block, 0])
         hidden = jnp.maximum(hidden + offset_ref[block, 0:1, :], 0.0)
-        mixed = product(split_bf16(hidden), (mix_ref[block, 1, 0], mix_ref[block, 1, 1]))
+        mixed = times(hidden, mix_ref[block, 1])
         mixed = soft_shrink(mixed + offset_ref[block, 1:2, :])
         mixed = jnp.concatenate(
             [mixed[wave * latitudes : (wave + 1) * latitudes] for wave in range(each)], axis=1
         )
-        turned_back = product((back_ref[0], back_ref[1]), split_bf16(mixed))
+        turned_back = times(back_ref[...], mixed)
         for wave in range(each):
             parts = combine(turned_back, wave, -1.0)
             for part in range(3):
@@ -417,7 +396,7 @@
                 ],
                 axis=0,
             ).astype(jnp.bfloat16)
-            restored = product((inverse_ref[0], inverse_ref[1]), (right,))
+            restored = times(inverse_ref[...], right)
             result = tokens(block, lat) + restored + normed[lat]
             for s in range(4):
                 piece = result[s * quarter : (s + 1) * quarter]
@@ -471,7 +450,7 @@
             slices = [token[block, s, which_quarter, lat].astype(jnp.float32) for s in range(4)]
             stream[lat * quarter : (lat + 1) * quarter] = lanes_of(slices)
         values = stream[...]
-        normal = layer_norm(values, second_ref[block, 0:1, :], second_ref[block, 1:2, :])
+        normal = layer_norm(values, order_ref[block, 1:2, :], order_ref[block, 3:4, :])
         normal = normal.astype(jnp.bfloat16)
         wide = w_in.shape[3]
         for part in range(2):
@@ -490,11 +469,62 @@
         total = total + jnp.dot(
             hidden_ref[:, wide:], w_out[block, 1], preferred_element_type=jnp.float32
         )
-        return reorder(total)
+        total_ref[...] = reorder(total)
+
+    zeros = functools.partial(jnp.zeros, dtype=jnp.float32)
+    for block in range(2):
+        both = jnp.concatenate([gain_ref[block], shift_ref[block], zeros((4, 4 * slot))], axis=0)
+        order_ref[block] = reorder(both)
+        head = order_ref[block, :, pl.ds(pl.multiple_of(mine * 128, 128), 128)]
+        tail = order_ref[block, :, pl.ds(pl.multiple_of(512 + comp * 128, 128), 128)]
+        tail = jnp.where(tile == 0, tail, swap(tail))
+        tail = jnp.where(first_half, tail, swap(tail))
+        affine_ref[block] = jnp.concatenate([head, tail], axis=1)
+        for sublayer in range(2):
+
+            def placed(weight):
+                width = weight.shape[1]
+                wide = jnp.concatenate([weight, zeros((slot, 128 - width))], axis=1)
+                moved = pltpu.roll(wide[width:], width, 1)
+                low = jnp.where(lane >= width, moved, 0.0)
+                high = jnp.where(first_half, moved, 0.0)
+                return (
+                    jnp.concatenate([wide[:width], low], axis=0),
+                    jnp.concatenate([zeros((width, 128)), high], axis=0),
+                )
+
+            real, real_tail = placed(weight_ref[block, sublayer, 0])
+            imag, imag_tail = placed(weight_ref[block, sublayer, 1])
+            upper = jnp.concatenate([real, imag, real_tail + swap(imag_tail)], axis=1)
+            lower = jnp.concatenate([-imag, real, swap(real_tail) - imag_tail], axis=1)
+            mix_ref[block, sublayer] = jnp.concatenate(
+                [upper[:128], lower[:128], upper[128:], lower[128:]], axis=0
+            ).astype(jnp.bfloat16)
+            bias = bias_ref[block, sublayer]
+            tail = jnp.concatenate([bias[:, 128:], bias[:, 128:]], axis=1)
+            offset_ref[block, sublayer : sublayer + 1, :] = jnp.concatenate(
+                [bias[0:1, :128], bias[1:2, :128], jnp.where(first_half, tail[0:1], tail[1:2])], axis=1
+            )
+    share_ref[...] = zeros(share_ref.shape)
+    heads = jnp.concatenate([flux_head_ref[...].astype(jnp.float32), zeros((slot, 120))], axis=1)
+    heads = jnp.concatenate([heads, zeros((256 - slot, 128))], axis=0).T
+    share_ref[0:8, :] = heads[:8]
+    for f in range(4):
+        for a in range(2):
+            for e in range(2):
+                at, row = 8 + e * 16 + a * 8 + f, f * 4 + a * 2 + e
+                share_ref[at : at + 1, :slot] = patch_ref[row : row + 1, :]
+    mask_ref[...] = zeros(mask_ref.shape)
+    mask_ref[: 2 * rows, :cells] = sea_ref[...].astype(jnp.float32)
+    level_ref[...] = zeros(level_ref.shape)
+    for level in range(rows + 4):
+        level_ref[level * 8 : level * 8 + 8, level * 256 : (level + 1) * 256] = flux_embed_ref[...]
+    spread_ref[0], spread_ref[1] = split_bf16(level_ref[...])
+    fields = jnp.concatenate([field_head_ref[...], zeros((256, 124))], axis=1).T
+    field_ref[...] = jnp.concatenate(thirds(fields[:8]), axis=0)
 
     spectral_filter(0)
     team_finish(share_ref, shared_ref, sent_share, came_share, "whole")
-    half_out[...] = mlp(0, 1 - comp).astype(jnp.bfloat16)
     copy = pltpu.make_async_remote_copy(
         src_ref=half_out,
         dst_ref=half_in,
@@ -503,10 +533,20 @@
         device_id={"comp": 1 - comp},
         device_id_type=MESH,
     )
-    copy.start()
-    total = mlp(0, comp)
+
+    def halves(i, carry):
+        mlp(0, lax.rem(1 - comp + i, 2))
+
+        @pl.when(i == 0)
+        def _():
+            half_out[...] = total_ref[...].astype(jnp.bfloat16)
+            copy.start()
+
+        return carry
+
+    lax.fori_loop(0, 2, halves, 0)
     copy.wait()
-    first = stream[...] + total + half_in[...].astype(jnp.float32)
+    first = stream[...] + total_ref[...] + half_in[...].astype(jnp.float32)
     first = first.astype(jnp.bfloat16)
     stream[...] = first.astype(jnp.float32)
 
@@ -584,7 +624,7 @@
                     values = tile_ref[part, row, pl.ds(at + 5 + e, 16), :]
                     for a in range(7):
                         if 0 <= row - a < 2 * rows:
-                            tap = depth_ref[a * 7 + e : a * 7 + e + 1, span]
+                            tap = depth_ref[a, e : e + 1, span]
                             totals[row - a] = totals[row - a] + values * tap
             for row in range(2 * rows):
                 conv_ref[row, pl.ds(at, 16), span] = totals[row]
@@ -595,7 +635,7 @@
     own_columns = jnp.concatenate([mask_ref[...], jnp.zeros((120, 256), jnp.float32)], axis=0).T
     for start_row in range(0, 2 * rows, 2):
         values = conv_ref[start_row : start_row + 2].reshape(2 * cells, 256)
-        normal = layer_norm(values, ocean_affine_ref[0:1, :], ocean_affine_ref[1:2, :])
+        normal = layer_norm(values, ocean_gain_ref[...], ocean_shift_ref[...])
         normal = normal.astype(jnp.bfloat16)
 
         def piece(i, carry):
@@ -606,7 +646,7 @@
 
         lax.fori_loop(0, ocean_in_ref.shape[1] // 256, piece, 0)
         update = jnp.dot(wave_ref[...], ocean_out_ref[...], preferred_element_type=jnp.float32)
-        update = update * ocean_affine_ref[2:3, :]
+        update = update * layer_ref[...]
         for row in range(start_row, start_row + 2):
             begin = jnp.concatenate([tile_ref[part, row + 3, 8 : 8 + cells] for part in range(2)], axis=1)
             change = update[(row - start_row) * cells : (row - start_row + 1) * cells]
@@ -633,11 +673,12 @@
     team_finish(*args)
 
     spectral_filter(1)
-    for which_quarter in range(2):
-        total = mlp(1, which_quarter)
+
+    def quarters(which_quarter, carry):
+        mlp(1, which_quarter)
         for lat in range(rows):
             pack(
-                total[lat * quarter : (lat + 1) * quarter],
+                total_ref[lat * quarter : (lat + 1) * quarter],
                 lambda s, lat=lat: part_out.at[which_quarter, s, lat],
             )
         team_exchange(
@@ -645,6 +686,9 @@
             sent_part.at[which_quarter], came_part.at[which_quarter], "each",
         )
         part_in[which_quarter, mine] = part_out[which_quarter, mine]
+        return carry
+
+    lax.fori_loop(0, 2, quarters, 0)
     for which_quarter in range(2):
         team_finish(
             part_out.at[which_quarter], part_in.at[which_quarter],
@@ -669,7 +713,6 @@
     ocean_state, sea_mask, depth_kernel, ocean_gain, ocean_shift, ocean_in, ocean_out, layer_scale,
     field_head, patch_embed,
 ):
-    column_index = lax.axis_index(("comp", "tile"))
     bands = lax.axis_size("band")
     rows, longitudes, slot = atmosphere.shape
     quarter = longitudes // 4
@@ -680,42 +723,15 @@
     cells, ocean_channels = ocean_state.shape[1:]
     waves = ocean_in.shape[1]
 
-    def heads_first(array):
-        split = array.reshape(array.shape[:-1] + (4, slot))
-        lead = array.shape[:-1]
-        return jnp.concatenate(
-            [split[..., :128].reshape(lead + (-1,)), split[..., 128:].reshape(lead + (-1,))], axis=-1
-        )
-
-    def taller(array, height):
-        return jnp.pad(array, ((0, 0),) * (array.ndim - 2) + ((0, height - array.shape[-2]), (0, 0)))
-
-    affine = jnp.stack([norm_gain[:, 0], norm_shift[:, 0]], axis=1)
-    affine = lax.dynamic_slice_in_dim(affine, column_index * slot, slot, axis=2)
-    affine = taller(jnp.concatenate([affine, affine[:, :, 128:]], axis=2), 8)
-    second = taller(heads_first(jnp.stack([norm_gain[:, 1], norm_shift[:, 1]], axis=1)), 8)
-    mixes = [mix_matrices(spec_weight[b], spec_bias[b]) for b in range(2)]
-    mix = jnp.stack([m[0] for m in mixes])
-    offsets = jnp.stack([m[1] for m in mixes])
-    patch = patch_embed.reshape(4, 2, 2, slot).transpose(2, 1, 0, 3)
-    patch = jnp.pad(patch, ((0, 0), (0, 0), (0, 4), (0, 0))).reshape(32, slot)
-    share = jnp.concatenate([flux_head.astype(jnp.float32).T, patch], axis=0)
-    share = jnp.pad(share, ((0, 0), (0, 256 - slot)))
-    mask = jnp.pad(sea_mask.astype(jnp.float32), ((0, 8 - sea_mask.shape[0]), (0, 256 - cells)))
-    levels = rows + 4
-    embed = jnp.eye(levels)[:, None, :, None] * flux_embed[None, :, None, :]
-    embed = taller(embed.reshape(levels * 8, levels * ocean_channels), 128)
-    embed = jnp.stack(split_bf16(embed))
-    depth = taller(depth_kernel.reshape(49, ocean_channels), 56)
-    ocean_affine = taller(jnp.stack([ocean_gain, ocean_shift, layer_scale]), 8)
-    field = jnp.concatenate([jnp.pad(f, ((0, 4), (0, 0))) for f in thirds(field_head.T)], axis=0)
     inside, outside = pl.BlockSpec(memory_space=pltpu.VMEM), pl.BlockSpec(memory_space=pl.ANY)
     arguments = [
-        atmosphere, affine, *transforms(latitudes, longitudes, bands), mix, offsets, second,
-        fc_in, fc_out, share, ocean_state, mask, embed, depth, ocean_affine, ocean_in, ocean_out,
-        field, *ocean_selectors(quarter),
+        atmosphere, spec_weight, spec_bias, norm_gain, norm_shift, fc_in, fc_out, flux_head,
+        flux_embed, ocean_state, sea_mask, depth_kernel, ocean_gain[None], ocean_shift[None],
+        ocean_in, ocean_out, layer_scale[None], field_head, patch_embed,
+        *transforms(latitudes, longitudes, bands), *ocean_selectors(quarter),
     ]
-    specs = [inside] * 9 + [outside] * 2 + [inside] * (len(arguments) - 11)
+    specs = [inside] * 5 + [outside] * 2 + [inside] * (len(arguments) - 7)
+    levels = (rows + 4) * ocean_channels
     narrow, single = jnp.bfloat16, jnp.float32
 
     def dma(*shape):
@@ -742,11 +758,11 @@
         pltpu.VMEM((count, channels), narrow),
         pltpu.VMEM((2, 4, rows, packed, 128), narrow),
         pltpu.VMEM((2, 4, rows, packed, 128), narrow),
-        pltpu.VMEM((4,) + share.shape, single),
+        pltpu.VMEM((4, 40, 256), single),
         pltpu.VMEM((2, 3, cells, ocean_channels), narrow),
         pltpu.VMEM((2, 2 * rows, 16, ocean_channels), narrow),
         pltpu.VMEM((2, 2, 3, 16, ocean_channels), narrow),
-        pltpu.VMEM((8,) + mask.shape, single),
+        pltpu.VMEM((8, 8, 256), single),
         pltpu.VMEM((rows, 8, 128), single),
         pltpu.VMEM((8, rows, 8, 128), single),
         pltpu.VMEM((2, 2 * rows + 6, cells + 16, 128), single),
@@ -754,6 +770,16 @@
         pltpu.VMEM((2 * cells, waves), narrow),
         pltpu.VMEM((4, rows, packed, 128), narrow),
         pltpu.VMEM((4, rows, packed, 128), narrow),
+        pltpu.VMEM((2, 8, channels), single),
+        pltpu.VMEM((2, 8, 256), single),
+        pltpu.VMEM((2, 2, 2 * slot, 2 * slot), narrow),
+        pltpu.VMEM((2, 8, 2 * slot), single),
+        pltpu.VMEM((40, 256), single),
+        pltpu.VMEM((8, 256), single),
+        pltpu.VMEM((128, levels), single),
+        pltpu.VMEM((2, 128, levels), narrow),
+        pltpu.VMEM((24, ocean_channels), narrow),
+        pltpu.VMEM((count, channels), single),
         dma(2, 4), dma(2, 4), dma(2, bands), dma(2, bands), dma(2, bands), dma(2, bands),
         dma(2, 4), dma(2, 4), dma(1), dma(1), dma(2, 4), dma(2, 4), dma(2, 2), dma(2, 2), dma(2, 2),
         dma(4), dma(4), dma(8), dma(8), dma(8), dma(8), dma(8), dma(8), dma(4), dma(4),

time: 210 us -> 192 us (0.914)
  Pallas kernels: 189 us -> 180 us
  other arithmetic: 8.41 us -> 0 us
    pallas_call x1, Pallas kernels: 189 us -> 180 us  [on_device(): pl.pallas_call(functools.partial(step_kernel, bands), out_shape=(jax.Shap...]
    unnamed x31 -> x5, local copies, waits for them, and re-layouts: 4.07 us -> 8.94 us
    another operation x9 -> x0, other arithmetic: 4.26 us -> none  [the longest x2 1.81 us: on_device(): mix = jnp.stack([m[0] for m in mixes])]
    concatenate x8 -> x0, other arithmetic: 3.21 us -> none  [the longest x1 0.68 us: on_device(): affine = taller(jnp.concatenate([affine, affine[:, :, 128:]], axis=2), 8)]
where the time goes in v2:
time: 192 us; the launch traced here: 191 us
  Pallas kernels  180 us (94%)
  local copies, waits for them, and re-layouts  10.3 us (5%)
    pallas_call x1, Pallas kernels, on_device(): pl.pallas_call(functools.partial(step_kernel, bands), out_shape=(jax.Shap...  180 us
    unnamed x5, local copies, waits for them, and re-layouts  8.94 us

profile of v2, /device:TPU:1, one launch (start us, length us, event | category | flops | bytes accessed | tf_op | source)
XLA Modules:
  0.0 191.3 jit_solution(15705751032484625685)
XLA Ops:
  0.6 1.4 copy.30.refs_7_
  2.0 1.5 copy.31.refs_17_
  3.5 2.1 %copy.29.refs_0_ = bf16[3,384,192]{2,1,0:T(8,128)(2,1)} copy(bf16[3,384,192]{1,2,0:T(8,128)(2,1)} %param.26) | data formatting | bytes 884736 | tf_op args[0]
  5.6 180.3 %shard_map.265 = (bf16[3,384,192]{2,1,0:T(8,128)(2,1)}, bf16[6,192,256]{2,1,0:T(8,128)(2,1)}, f32[6,8,192]{2,1,0:T(8,128)}) custom-call(bf16[3,384,192]{2,1,0:T(8,128)(2,1)} %copy.29.refs_0_, f32[2,2,2,192,96]{4,3,2,1,0:T(8,128)} %refs_1_.1, f32[2,2,2,192]{3,2,1,0:T(2,128)} %refs_2_.1, f32[2,2,768]{2,1,0:T(2,128)} %refs_3_.1, f32[2,2,768]{2,1,0:T(2,128)} %refs_4_.1, ...), custom_call_target="tpu_custom_call" | custom-call | tf_op jit(solution)/shard_map/pallas_call | solution.py:787
  185.9 2.1 %copy.32 = bf16[3,384,192]{1,2,0:T(8,128)(2,1)} copy(bf16[3,384,192]{2,1,0:T(8,128)(2,1)} %get-tuple-element.9) | data formatting | bytes 884736
  188.0 1.4 slice_bitcast_fusion
  189.4 1.9 %copy.34 = bf16[6,192,256]{2,1,0:T(8,128)(2,1)} copy(bf16[6,192,256]{2,1,0:T(8,128)(2,1)} %get-tuple-element.16) | data formatting | bytes 1179648

commit v3 on v2

--- a/solution.py
+++ b/solution.py
@@ -114,13 +114,13 @@
         w_in, w_out, stream, hidden_ref, half_out, half_in, part_out, part_in, shared_ref,
         rows_in, cols_in, corner_in, masks_in, flux_ref, flux_in, tile_ref, conv_ref, wave_ref,
         middle_out, middle_in, order_ref, affine_ref, mix_ref, offset_ref, share_ref, mask_ref,
-        level_ref, spread_ref, field_ref, total_ref,
+        level_ref, spread_ref, field_ref, total_ref, turned_ref, flat_ref, near_sums, all_near,
         sent_sum, came_sum, sent_a, came_a, sent_b, came_b, sent_out, came_out,
         sent_half, came_half, sent_part, came_part, load, sent_load, came_load,
         sent_share, came_share, sent_cells, came_cells, sent_mask, came_mask, sent_flux, came_flux,
-        sent_middle, came_middle,
+        sent_middle, came_middle, sent_near, came_near,
     ) = refs
-    rows, longitudes, slot = x_ref.shape
+    rows, slot, longitudes = x_ref.shape
     quarter = longitudes // 4
     middle = quarter // 2
     latitudes = rows * bands
@@ -226,8 +226,7 @@
 
     def team_copy(source, target, sent, came, step, pick, landing):
         index = member(step)
-        chosen = {"whole": lambda: source, "half": lambda: source.at[lax.rem(index, 2)],
-                  "each": lambda: source.at[index]}[pick]()
+        chosen = {"whole": lambda: source, "each": lambda: source.at[index]}[pick]()
         place = index if landing else mine
         return pltpu.make_async_remote_copy(
             src_ref=chosen,
@@ -245,6 +244,19 @@
     def team_finish(source, target, sent, came, pick):
         for step in range(1, 4):
             team_copy(source, target, sent, came, step, pick, True).wait()
+
+    def out_copy(block, turn, step, landing):
+        index = member(step)
+        place = index if landing else mine
+        wanted = lax.rem(1 - (comp if landing else lax.div(index, 2)) + turn, 2)
+        return pltpu.make_async_remote_copy(
+            src_ref=after.at[lax.rem(index, 2), wanted],
+            dst_ref=token.at[block, place, wanted],
+            send_sem=sent_out.at[block, turn, index],
+            recv_sem=came_out.at[block, turn, place],
+            device_id=team_id(index),
+            device_id_type=MESH,
+        )
 
     def band_copy(source, target, sent, came, step, landing):
         index = lax.rem(me + step, bands)
@@ -278,8 +290,7 @@
     first_half = lane < slot - 128
     sign = jnp.where(first_half, 1.0, -1.0)
     half = longitudes // 2
-    counted = jnp.where(lax.broadcasted_iota(jnp.int32, (8, 256), 1) < slot, 1.0, 0.0)
-    counted = counted.astype(jnp.bfloat16)
+    counted = jnp.ones((8, slot), jnp.bfloat16)
     which = lax.broadcasted_iota(jnp.int32, (8, longitudes), 0)
     turned = (((1,), (1,)), ((), ()))
 
@@ -296,8 +307,7 @@
 
     def tokens(block, lat):
         if block == 0:
-            values = x_ref[lat].astype(jnp.float32)
-            return jnp.concatenate([values, values[:, 128:]], axis=1)
+            return turned_ref[lat]
         pieces = [middle_in[s, lat].astype(jnp.float32) for s in range(4)]
         return jnp.concatenate(
             [jnp.concatenate([p[:quarter], doubled(p[quarter:])], axis=1) for p in pieces], axis=0
@@ -310,31 +320,32 @@
         return landed[pl.ds(part * 9 + lat * 3 + wave, bands, stride=32), :]
 
     def spectral_filter(block):
-        total = jnp.zeros((8, longitudes), jnp.float32)
-        for lat in range(rows):
-            values = tokens(block, lat)
-            high, low = split_bf16(values * values)
-            total = total + jnp.where(
-                which == lat, across_rows(counted, values.astype(jnp.bfloat16)), 0.0
-            )
-            total = total + jnp.where(
-                which == rows + lat, across_rows(counted, high) + across_rows(counted, low), 0.0
-            )
-        sums[...] = total
         if block == 0:
+            total = jnp.zeros((8, longitudes), jnp.float32)
+            for lat in range(rows):
+                values = x_ref[lat].astype(jnp.float32)
+                high, low = split_bf16(values * values)
+                total = total + jnp.where(which == lat, times(counted, x_ref[lat]), 0.0)
+                total = total + jnp.where(
+                    which == rows + lat, times(counted, high) + times(counted, low), 0.0
+                )
+            sums[...] = total
             pl.semaphore_wait(barrier, bands - 1 + 3 + 4)
-        team_exchange(sums, all_sums.at[block], sent_sum.at[block], came_sum.at[block], "whole")
-        if block == 0:
+            team_exchange(sums, all_sums, sent_sum, came_sum, "whole")
             for copy in near_copies(*mask_args) + near_copies(*cell_args) + sibling_loads:
                 copy.start()
             team_exchange(share_ref, shared_ref, sent_share, came_share, "whole")
             shared_ref[mine] = share_ref[...]
-        all_sums[block, mine] = total
-        team_finish(sums, all_sums.at[block], sent_sum.at[block], came_sum.at[block], "whole")
-        total = (
-            all_sums[block, 0] + all_sums[block, 1] + all_sums[block, 2] + all_sums[block, 3]
-        ) * (1.0 / (4 * slot))
-        columns = jnp.concatenate([total, jnp.zeros((120, longitudes), jnp.float32)], axis=0).T
+            all_sums[mine] = total
+            team_finish(sums, all_sums, sent_sum, came_sum, "whole")
+            total = all_sums[0] + all_sums[1] + all_sums[2] + all_sums[3]
+            columns = jnp.concatenate([total, jnp.zeros((120, longitudes), jnp.float32)], axis=0).T
+        else:
+            blank = jnp.zeros((120, 128), jnp.float32)
+            columns = jnp.concatenate(
+                [jnp.concatenate([all_near[s], blank], axis=0).T[:quarter] for s in range(4)], axis=0
+            )
+        columns = columns * (1.0 / (4 * slot))
         for lat in range(rows):
             average = columns[:, lat : lat + 1]
             power = columns[:, rows + lat : rows + lat + 1]
@@ -404,10 +415,10 @@
                 tail = jnp.where(first_half, tail[:middle], swap(tail[middle:]))
                 after[s % 2, s // 2, lat, :quarter] = piece[:, :128].astype(jnp.bfloat16)
                 after[s % 2, s // 2, lat, quarter:] = tail.astype(jnp.bfloat16)
-        args = (after, token.at[block], sent_out.at[block], came_out.at[block], "half")
-        team_exchange(*args)
+        for turn in range(2):
+            for step in range(1, 4):
+                out_copy(block, turn, step, False).start()
         token[block, mine] = after[tile]
-        team_finish(*args)
         for i in range(2):
             own_loads[2 * block + i].wait()
             sibling_loads[2 * block + i].wait()
@@ -506,9 +517,10 @@
                 [bias[0:1, :128], bias[1:2, :128], jnp.where(first_half, tail[0:1], tail[1:2])], axis=1
             )
     share_ref[...] = zeros(share_ref.shape)
-    heads = jnp.concatenate([flux_head_ref[...].astype(jnp.float32), zeros((slot, 120))], axis=1)
-    heads = jnp.concatenate([heads, zeros((256 - slot, 128))], axis=0).T
-    share_ref[0:8, :] = heads[:8]
+    share_ref[0:8, :slot] = flux_head_ref[...].astype(jnp.float32)
+    for lat in range(rows):
+        values = x_ref[lat].astype(jnp.float32)
+        turned_ref[lat] = jnp.concatenate([values, values[128:]], axis=0).T
     for f in range(4):
         for a in range(2):
             for e in range(2):
@@ -520,8 +532,8 @@
     for level in range(rows + 4):
         level_ref[level * 8 : level * 8 + 8, level * 256 : (level + 1) * 256] = flux_embed_ref[...]
     spread_ref[0], spread_ref[1] = split_bf16(level_ref[...])
-    fields = jnp.concatenate([field_head_ref[...], zeros((256, 124))], axis=1).T
-    field_ref[...] = jnp.concatenate(thirds(fields[:8]), axis=0)
+    fields = jnp.concatenate([field_head_ref[...], zeros((4, 256))], axis=0)
+    field_ref[...] = jnp.concatenate(thirds(fields), axis=0)
 
     spectral_filter(0)
     team_finish(share_ref, shared_ref, sent_share, came_share, "whole")
@@ -535,6 +547,8 @@
     )
 
     def halves(i, carry):
+        for step in range(1, 4):
+            out_copy(0, i, step, True).wait()
         mlp(0, lax.rem(1 - comp + i, 2))
 
         @pl.when(i == 0)
@@ -654,10 +668,12 @@
             next_ref[row] = fresh
             field = across_rows(field_ref[...], fresh)
             field = (field[:8] + field[8:16] + field[16:24]) * mask_ref[row : row + 1, :cells]
-            surface_ref[row] = field
-
+            flat_ref[row] = field
+            surface_ref[row] = field[:4]
+
+    near = zeros((8, quarter))
     for lat in range(rows):
-        both = jnp.concatenate([surface_ref[2 * lat], surface_ref[2 * lat + 1]], axis=0)
+        both = jnp.concatenate([flat_ref[2 * lat], flat_ref[2 * lat + 1]], axis=0)
         patch = across_rows(split_ref[...], jnp.concatenate(thirds(both), axis=0))
         patch = patch[:, :16] + patch[:, 16:32] + patch[:, 32:48]
         total = stream[lat * quarter : (lat + 1) * quarter]
@@ -667,14 +683,30 @@
                 split_bf16(embed[e * 16 : (e + 1) * 16]),
             )
         pack(total, lambda s, lat=lat: middle_out.at[s, lat])
+        rounded = total.astype(jnp.bfloat16)
+        wide = rounded.astype(jnp.float32)
+        high, low = split_bf16(wide * wide)
+        every = jnp.ones((8, 4 * slot), jnp.bfloat16)
+        plain, power = across_rows(every, rounded), across_rows(every, high) + across_rows(every, low)
+        row_index = lax.broadcasted_iota(jnp.int32, (8, quarter), 0)
+        near = near + jnp.where(row_index == lat, plain, 0.0)
+        near = near + jnp.where(row_index == rows + lat, power, 0.0)
+    near_sums[...] = jnp.concatenate([near, zeros((8, 128 - quarter))], axis=1)
+    near_args = (near_sums, all_near, sent_near, came_near, "whole")
+    team_exchange(*near_args)
+    all_near[mine] = near_sums[...]
     args = (middle_out, middle_in, sent_middle, came_middle, "each")
     team_exchange(*args)
     middle_in[mine] = middle_out[mine]
     team_finish(*args)
+    team_finish(*near_args)
 
     spectral_filter(1)
 
-    def quarters(which_quarter, carry):
+    def quarters(i, carry):
+        for step in range(1, 4):
+            out_copy(1, i, step, True).wait()
+        which_quarter = lax.rem(1 - comp + i, 2)
         mlp(1, which_quarter)
         for lat in range(rows):
             pack(
@@ -725,9 +757,10 @@
 
     inside, outside = pl.BlockSpec(memory_space=pltpu.VMEM), pl.BlockSpec(memory_space=pl.ANY)
     arguments = [
-        atmosphere, spec_weight, spec_bias, norm_gain, norm_shift, fc_in, fc_out, flux_head,
+        atmosphere.transpose(0, 2, 1), spec_weight, spec_bias, norm_gain, norm_shift, fc_in, fc_out,
+        flux_head.T,
         flux_embed, ocean_state, sea_mask, depth_kernel, ocean_gain[None], ocean_shift[None],
-        ocean_in, ocean_out, layer_scale[None], field_head, patch_embed,
+        ocean_in, ocean_out, layer_scale[None], field_head.T, patch_embed,
         *transforms(latitudes, longitudes, bands), *ocean_selectors(quarter),
     ]
     specs = [inside] * 5 + [outside] * 2 + [inside] * (len(arguments) - 7)
@@ -745,7 +778,7 @@
         pltpu.VMEM((bands * 32, 128), single),
         pltpu.VMEM((bands * 32, 128), single),
         pltpu.VMEM((8, longitudes), single),
-        pltpu.VMEM((2, 4, 8, longitudes), single),
+        pltpu.VMEM((4, 8, longitudes), single),
         pltpu.VMEM(chunks, narrow),
         pltpu.VMEM((2,) + chunks, narrow),
         pltpu.VMEM(chunks, narrow),
@@ -780,16 +813,21 @@
         pltpu.VMEM((2, 128, levels), narrow),
         pltpu.VMEM((24, ocean_channels), narrow),
         pltpu.VMEM((count, channels), single),
-        dma(2, 4), dma(2, 4), dma(2, bands), dma(2, bands), dma(2, bands), dma(2, bands),
-        dma(2, 4), dma(2, 4), dma(1), dma(1), dma(2, 4), dma(2, 4), dma(2, 2), dma(2, 2), dma(2, 2),
+        pltpu.VMEM((rows, longitudes, 256), single),
+        pltpu.VMEM((2 * rows, 8, cells), single),
+        pltpu.VMEM((8, 128), single),
+        pltpu.VMEM((4, 8, 128), single),
+        dma(4), dma(4), dma(2, bands), dma(2, bands), dma(2, bands), dma(2, bands),
+        dma(2, 2, 4), dma(2, 2, 4), dma(1), dma(1), dma(2, 4), dma(2, 4), dma(2, 2), dma(2, 2), dma(2, 2),
         dma(4), dma(4), dma(8), dma(8), dma(8), dma(8), dma(8), dma(8), dma(4), dma(4),
+        dma(4), dma(4),
     ]
     atmosphere_next, ocean_next, surface = pl.pallas_call(
         functools.partial(step_kernel, bands),
         out_shape=(
             jax.ShapeDtypeStruct(atmosphere.shape, narrow),
             jax.ShapeDtypeStruct(ocean_state.shape, narrow),
-            jax.ShapeDtypeStruct((2 * rows, 8, cells), single),
+            jax.ShapeDtypeStruct((2 * rows, 4, cells), single),
         ),
         in_specs=specs,
         out_specs=(inside,) * 3,
@@ -798,7 +836,7 @@
             collective_id=0, has_side_effects=True, vmem_limit_bytes=63 << 20
         ),
     )(*arguments)
-    return (atmosphere_next, ocean_next, surface[:, :4].transpose(0, 2, 1))
+    return (atmosphere_next, ocean_next, surface.transpose(0, 2, 1))
 
 
 def solution(mesh):

time: 192 us -> 178 us (0.927)
  Pallas kernels: 180 us -> 171 us
  local copies, waits for them, and re-layouts: 10.3 us -> 5.32 us
    pallas_call x1, Pallas kernels: 180 us -> 171 us  [on_device(): pl.pallas_call(functools.partial(step_kernel, bands), out_shape=(jax.Shap...]
    unnamed x5 -> x3, local copies, waits for them, and re-layouts: 8.94 us -> 5.32 us
where the time goes in v3:
time: 178 us; the launch traced here: 176 us
  Pallas kernels  171 us (96%)
  local copies, waits for them, and re-layouts  5.32 us (3%)
    pallas_call x1, Pallas kernels, on_device(): pl.pallas_call(functools.partial(step_kernel, bands), out_shape=(jax.Shap...  171 us
    unnamed x3, local copies, waits for them, and re-layouts  5.32 us

profile of v3, /device:TPU:1, one launch (start us, length us, event | category | flops | bytes accessed | tf_op | source)
XLA Modules:
  0.0 176.5 jit_solution(1916606668255748930)
XLA Ops:
  0.6 170.5 %shard_map.265 = (bf16[3,384,192]{2,1,0:T(8,128)(2,1)}, bf16[6,192,256]{2,1,0:T(8,128)(2,1)}, f32[6,4,192]{2,1,0:T(4,128)}) custom-call(bf16[3,192,384]{2,1,0:T(8,128)(2,1)} %bitcast.7, f32[2,2,2,192,96]{4,3,2,1,0:T(8,128)} %refs_1_.1, f32[2,2,2,192]{3,2,1,0:T(2,128)} %refs_2_.1, f32[2,2,768]{2,1,0:T(2,128)} %refs_3_.1, f32[2,2,768]{2,1,0:T(2,128)} %refs_4_.1, ...), custom_call_target="tpu_custom_call" | custom-call | tf_op jit(solution)/shard_map/pallas_call | solution.py:825
  171.2 2.1 %copy.29 = bf16[3,384,192]{1,2,0:T(8,128)(2,1)} copy(bf16[3,384,192]{2,1,0:T(8,128)(2,1)} %get-tuple-element.9) | data formatting | bytes 884736
  173.2 1.9 %copy.32 = bf16[6,192,256]{2,1,0:T(8,128)(2,1)} copy(bf16[6,192,256]{2,1,0:T(8,128)(2,1)} %get-tuple-element.16) | data formatting | bytes 1179648
  175.1 1.3 copy.33

commit v4 on v3

--- a/solution.py
+++ b/solution.py
@@ -115,6 +115,7 @@
         rows_in, cols_in, corner_in, masks_in, flux_ref, flux_in, tile_ref, conv_ref, wave_ref,
         middle_out, middle_in, order_ref, affine_ref, mix_ref, offset_ref, share_ref, mask_ref,
         level_ref, spread_ref, field_ref, total_ref, turned_ref, flat_ref, near_sums, all_near,
+        seen_masks, own_masks,
         sent_sum, came_sum, sent_a, came_a, sent_b, came_b, sent_out, came_out,
         sent_half, came_half, sent_part, came_part, load, sent_load, came_load,
         sent_share, came_share, sent_cells, came_cells, sent_mask, came_mask, sent_flux, came_flux,
@@ -248,7 +249,9 @@
     def out_copy(block, turn, step, landing):
         index = member(step)
         place = index if landing else mine
-        wanted = lax.rem(1 - (comp if landing else lax.div(index, 2)) + turn, 2)
+        wanted = turn
+        if block == 0:
+            wanted = lax.rem(1 - (comp if landing else lax.div(index, 2)) + turn, 2)
         return pltpu.make_async_remote_copy(
             src_ref=after.at[lax.rem(index, 2), wanted],
             dst_ref=token.at[block, place, wanted],
@@ -269,8 +272,8 @@
             device_id_type=MESH,
         )
 
-    def band_exchange(source, target, sent, came):
-        source[...] = stage[...].astype(jnp.bfloat16).reshape(source.shape)
+    def band_exchange(source, target, sent, came, meanwhile):
+        source[...] = stage[: bands * 32].astype(jnp.bfloat16).reshape(source.shape)
 
         def go(step, carry):
             band_copy(source, target, sent, came, step, False).start()
@@ -278,13 +281,20 @@
 
         lax.fori_loop(1, bands, go, 0)
         target[me] = source[me]
+        meanwhile()
+
+        def widen(index):
+            at = pl.multiple_of(index * 32, 32)
+            landed[pl.ds(at, 32), :] = target[index].astype(jnp.float32)
+
+        widen(me)
 
         def come(step, carry):
             band_copy(source, target, sent, came, step, True).wait()
+            widen(lax.rem(me + step, bands))
             return carry
 
         lax.fori_loop(1, bands, come, 0)
-        landed[...] = target[...].astype(jnp.float32).reshape(landed.shape)
 
     lane = lax.broadcasted_iota(jnp.int32, (1, 128), 1)
     first_half = lane < slot - 128
@@ -319,7 +329,7 @@
     def collect(lat, wave, part):
         return landed[pl.ds(part * 9 + lat * 3 + wave, bands, stride=32), :]
 
-    def spectral_filter(block):
+    def spectral_filter(block, while_first, while_second):
         if block == 0:
             total = jnp.zeros((8, longitudes), jnp.float32)
             for lat in range(rows):
@@ -360,7 +370,7 @@
             for part in range(3):
                 for wave in range(each):
                     spread(lat, wave, part, parts[part][wave * bands : (wave + 1) * bands])
-        band_exchange(send_a, got_a.at[block], sent_a.at[block], came_a.at[block])
+        band_exchange(send_a, got_a.at[block], sent_a.at[block], came_a.at[block], while_first)
         pieces = []
         for wave in range(each):
             for part in range(3):
@@ -394,7 +404,7 @@
             for part in range(3):
                 for lat in range(rows):
                     spread(lat, wave, part, parts[part][lat * bands : (lat + 1) * bands])
-        band_exchange(send_b, got_b.at[block], sent_b.at[block], came_b.at[block])
+        band_exchange(send_b, got_b.at[block], sent_b.at[block], came_b.at[block], while_second)
         for lat in range(rows):
             real, imag, rest = (
                 jnp.concatenate([collect(lat, wave, part) for wave in range(each)], axis=0)
@@ -491,31 +501,6 @@
         tail = jnp.where(tile == 0, tail, swap(tail))
         tail = jnp.where(first_half, tail, swap(tail))
         affine_ref[block] = jnp.concatenate([head, tail], axis=1)
-        for sublayer in range(2):
-
-            def placed(weight):
-                width = weight.shape[1]
-                wide = jnp.concatenate([weight, zeros((slot, 128 - width))], axis=1)
-                moved = pltpu.roll(wide[width:], width, 1)
-                low = jnp.where(lane >= width, moved, 0.0)
-                high = jnp.where(first_half, moved, 0.0)
-                return (
-                    jnp.concatenate([wide[:width], low], axis=0),
-                    jnp.concatenate([zeros((width, 128)), high], axis=0),
-                )
-
-            real, real_tail = placed(weight_ref[block, sublayer, 0])
-            imag, imag_tail = placed(weight_ref[block, sublayer, 1])
-            upper = jnp.concatenate([real, imag, real_tail + swap(imag_tail)], axis=1)
-            lower = jnp.concatenate([-imag, real, swap(real_tail) - imag_tail], axis=1)
-            mix_ref[block, sublayer] = jnp.concatenate(
-                [upper[:128], lower[:128], upper[128:], lower[128:]], axis=0
-            ).astype(jnp.bfloat16)
-            bias = bias_ref[block, sublayer]
-            tail = jnp.concatenate([bias[:, 128:], bias[:, 128:]], axis=1)
-            offset_ref[block, sublayer : sublayer + 1, :] = jnp.concatenate(
-                [bias[0:1, :128], bias[1:2, :128], jnp.where(first_half, tail[0:1], tail[1:2])], axis=1
-            )
     share_ref[...] = zeros(share_ref.shape)
     share_ref[0:8, :slot] = flux_head_ref[...].astype(jnp.float32)
     for lat in range(rows):
@@ -528,14 +513,59 @@
                 share_ref[at : at + 1, :slot] = patch_ref[row : row + 1, :]
     mask_ref[...] = zeros(mask_ref.shape)
     mask_ref[: 2 * rows, :cells] = sea_ref[...].astype(jnp.float32)
-    level_ref[...] = zeros(level_ref.shape)
-    for level in range(rows + 4):
-        level_ref[level * 8 : level * 8 + 8, level * 256 : (level + 1) * 256] = flux_embed_ref[...]
-    spread_ref[0], spread_ref[1] = split_bf16(level_ref[...])
-    fields = jnp.concatenate([field_head_ref[...], zeros((4, 256))], axis=0)
-    field_ref[...] = jnp.concatenate(thirds(fields), axis=0)
-
-    spectral_filter(0)
+    ext_rows = 2 * rows + 6
+
+    def prepare_products():
+        for block in range(2):
+            for sublayer in range(2):
+
+                def placed(weight):
+                    width = weight.shape[1]
+                    wide = jnp.concatenate([weight, zeros((slot, 128 - width))], axis=1)
+                    moved = pltpu.roll(wide[width:], width, 1)
+                    low = jnp.where(lane >= width, moved, 0.0)
+                    high = jnp.where(first_half, moved, 0.0)
+                    return (
+                        jnp.concatenate([wide[:width], low], axis=0),
+                        jnp.concatenate([zeros((width, 128)), high], axis=0),
+                    )
+
+                real, real_tail = placed(weight_ref[block, sublayer, 0])
+                imag, imag_tail = placed(weight_ref[block, sublayer, 1])
+                upper = jnp.concatenate([real, imag, real_tail + swap(imag_tail)], axis=1)
+                lower = jnp.concatenate([-imag, real, swap(real_tail) - imag_tail], axis=1)
+                mix_ref[block, sublayer] = jnp.concatenate(
+                    [upper[:128], lower[:128], upper[128:], lower[128:]], axis=0
+                ).astype(jnp.bfloat16)
+                bias = bias_ref[block, sublayer]
+                tail = jnp.concatenate([bias[:, 128:], bias[:, 128:]], axis=1)
+                offset_ref[block, sublayer : sublayer + 1, :] = jnp.concatenate(
+                    [bias[0:1, :128], bias[1:2, :128], jnp.where(first_half, tail[0:1], tail[1:2])], axis=1
+                )
+        level_ref[...] = zeros(level_ref.shape)
+        for level in range(rows + 4):
+            level_ref[level * 8 : level * 8 + 8, level * 256 : (level + 1) * 256] = flux_embed_ref[...]
+        spread_ref[0], spread_ref[1] = split_bf16(level_ref[...])
+        fields = jnp.concatenate([field_head_ref[...], zeros((4, 256))], axis=0)
+        field_ref[...] = jnp.concatenate(thirds(fields), axis=0)
+
+    def mask_rows(b, c):
+        whole = mask_ref[...] if (b, c) == (0, 0) else masks_in[directions.index((b, c))]
+        whole = whole[:, 128:] if c < 0 else whole[:, :128] if c > 0 else whole
+        return whole[2 * rows - 3 : 2 * rows] if b < 0 else whole[:3] if b > 0 else whole[: 2 * rows]
+
+    def prepare_masks():
+        for copy in near_landings(*mask_args) + near_landings(*cell_args):
+            copy.wait()
+        masks = jnp.concatenate(
+            [jnp.concatenate([mask_rows(b, c) for c in (-1, 0, 1)], axis=1) for b in (-1, 0, 1)]
+            + [jnp.zeros((16 - ext_rows, 512), jnp.float32)],
+            axis=0,
+        )
+        seen_masks[...] = across_rows(seen_ref[...], masks.astype(jnp.bfloat16))
+        own_masks[...] = jnp.concatenate([mask_ref[...], zeros((120, 256))], axis=0).T
+
+    spectral_filter(0, prepare_products, prepare_masks)
     team_finish(share_ref, shared_ref, sent_share, came_share, "whole")
     copy = pltpu.make_async_remote_copy(
         src_ref=half_out,
@@ -577,7 +607,7 @@
         flux_ref[lat] = jnp.concatenate([flux, jnp.zeros((8, 128 - quarter), jnp.float32)], axis=1)
     for copy in near_copies(*flux_args):
         copy.start()
-    for copy in near_landings(*mask_args) + near_landings(*cell_args) + near_landings(*flux_args):
+    for copy in near_landings(*flux_args):
         copy.wait()
 
     def flux_at(lat, c):
@@ -596,18 +626,6 @@
     raised = raised[:, :128] + raised[:, 128:256] + raised[:, 256:]
     forcing = product(split_bf16(raised), (spread_ref[0], spread_ref[1]))
 
-    def mask_rows(b, c):
-        whole = mask_ref[...] if (b, c) == (0, 0) else masks_in[directions.index((b, c))]
-        whole = whole[:, 128:] if c < 0 else whole[:, :128] if c > 0 else whole
-        return whole[2 * rows - 3 : 2 * rows] if b < 0 else whole[:3] if b > 0 else whole[: 2 * rows]
-
-    ext_rows = 2 * rows + 6
-    masks = jnp.concatenate(
-        [jnp.concatenate([mask_rows(b, c) for c in (-1, 0, 1)], axis=1) for b in (-1, 0, 1)]
-        + [jnp.zeros((16 - ext_rows, 512), jnp.float32)],
-        axis=0,
-    )
-    masks = across_rows(seen_ref[...], masks.astype(jnp.bfloat16))
     for row in range(ext_rows):
         b = -1 if row < 3 else 1 if row >= 2 * rows + 3 else 0
         at = row if b < 0 else row - 3 if b == 0 else row - 2 * rows - 3
@@ -619,7 +637,7 @@
         sources = [s.astype(jnp.float32) for s in sources]
         state = jnp.concatenate([sources[0][8:], sources[1], sources[2][:8]], axis=0)
         level = (row - 3) // 2 + 2
-        start = state + masks[:, row : row + 1] * forcing[:, level * 256 : (level + 1) * 256]
+        start = state + seen_masks[:, row : row + 1] * forcing[:, level * 256 : (level + 1) * 256]
         start = start.astype(jnp.bfloat16).astype(jnp.float32)
         if b:
             inside = jnp.where(me > 0, 1.0, 0.0) if b < 0 else jnp.where(me < bands - 1, 1.0, 0.0)
@@ -646,7 +664,6 @@
 
         lax.fori_loop(0, cells // 16, strip, 0)
 
-    own_columns = jnp.concatenate([mask_ref[...], jnp.zeros((120, 256), jnp.float32)], axis=0).T
     for start_row in range(0, 2 * rows, 2):
         values = conv_ref[start_row : start_row + 2].reshape(2 * cells, 256)
         normal = layer_norm(values, ocean_gain_ref[...], ocean_shift_ref[...])
@@ -664,7 +681,7 @@
         for row in range(start_row, start_row + 2):
             begin = jnp.concatenate([tile_ref[part, row + 3, 8 : 8 + cells] for part in range(2)], axis=1)
             change = update[(row - start_row) * cells : (row - start_row + 1) * cells]
-            fresh = (begin + own_columns[:cells, row : row + 1] * change).astype(jnp.bfloat16)
+            fresh = (begin + own_masks[:cells, row : row + 1] * change).astype(jnp.bfloat16)
             next_ref[row] = fresh
             field = across_rows(field_ref[...], fresh)
             field = (field[:8] + field[8:16] + field[16:24]) * mask_ref[row : row + 1, :cells]
@@ -701,12 +718,11 @@
     team_finish(*args)
     team_finish(*near_args)
 
-    spectral_filter(1)
-
-    def quarters(i, carry):
+    spectral_filter(1, lambda: None, lambda: None)
+
+    def quarters(which_quarter, carry):
         for step in range(1, 4):
-            out_copy(1, i, step, True).wait()
-        which_quarter = lax.rem(1 - comp + i, 2)
+            out_copy(1, which_quarter, step, True).wait()
         mlp(1, which_quarter)
         for lat in range(rows):
             pack(
@@ -775,8 +791,8 @@
         pltpu.VMEM((rows, longitudes, 256), single),
         pltpu.VMEM((2, 2, rows, packed, 128), narrow),
         pltpu.VMEM((2, 4, 2, rows, packed, 128), narrow),
-        pltpu.VMEM((bands * 32, 128), single),
-        pltpu.VMEM((bands * 32, 128), single),
+        pltpu.VMEM((bands * 32 + 32, 128), single),
+        pltpu.VMEM((bands * 32 + 32, 128), single),
         pltpu.VMEM((8, longitudes), single),
         pltpu.VMEM((4, 8, longitudes), single),
         pltpu.VMEM(chunks, narrow),
@@ -817,6 +833,8 @@
         pltpu.VMEM((2 * rows, 8, cells), single),
         pltpu.VMEM((8, 128), single),
         pltpu.VMEM((4, 8, 128), single),
+        pltpu.VMEM((cells + 16, 16), single),
+        pltpu.VMEM((256, 128), single),
         dma(4), dma(4), dma(2, bands), dma(2, bands), dma(2, bands), dma(2, bands),
         dma(2, 2, 4), dma(2, 2, 4), dma(1), dma(1), dma(2, 4), dma(2, 4), dma(2, 2), dma(2, 2), dma(2, 2),
         dma(4), dma(4), dma(8), dma(8), dma(8), dma(8), dma(8), dma(8), dma(4), dma(4),

time: 178 us -> 178 us (level)
  no operation moved by 1% of the time
where the time goes in v4:
time: 178 us; the launch traced here: 176 us
  Pallas kernels  170 us (96%)
  local copies, waits for them, and re-layouts  5.32 us (3%)
    pallas_call x1, Pallas kernels, on_device(): pl.pallas_call(functools.partial(step_kernel, bands), out_shape=(jax.Shap...  170 us
    unnamed x3, local copies, waits for them, and re-layouts  5.32 us

profile of v4, /device:TPU:1, one launch (start us, length us, event | category | flops | bytes accessed | tf_op | source)
XLA Modules:
  0.0 175.9 jit_solution(7628289755573403394)
XLA Ops:
  0.6 170.0 %shard_map.265 = (bf16[3,384,192]{2,1,0:T(8,128)(2,1)}, bf16[6,192,256]{2,1,0:T(8,128)(2,1)}, f32[6,4,192]{2,1,0:T(4,128)}) custom-call(bf16[3,192,384]{2,1,0:T(8,128)(2,1)} %bitcast.7, f32[2,2,2,192,96]{4,3,2,1,0:T(8,128)} %refs_1_.1, f32[2,2,2,192]{3,2,1,0:T(2,128)} %refs_2_.1, f32[2,2,768]{2,1,0:T(2,128)} %refs_3_.1, f32[2,2,768]{2,1,0:T(2,128)} %refs_4_.1, ...), custom_call_target="tpu_custom_call" | custom-call | tf_op jit(solution)/shard_map/pallas_call | solution.py:843
  170.6 2.1 %copy.29 = bf16[3,384,192]{1,2,0:T(8,128)(2,1)} copy(bf16[3,384,192]{2,1,0:T(8,128)(2,1)} %get-tuple-element.9) | data formatting | bytes 884736
  172.7 1.9 %copy.32 = bf16[6,192,256]{2,1,0:T(8,128)(2,1)} copy(bf16[6,192,256]{2,1,0:T(8,128)(2,1)} %get-tuple-element.16) | data formatting | bytes 1179648
  174.6 1.3 copy.33

commit v5 on v4

--- a/solution.py
+++ b/solution.py
@@ -246,23 +246,28 @@
         for step in range(1, 4):
             team_copy(source, target, sent, came, step, pick, True).wait()
 
-    def out_copy(block, turn, step, landing):
+    def out_copy(block, turn, lat, step, landing):
         index = member(step)
         place = index if landing else mine
         wanted = turn
         if block == 0:
             wanted = lax.rem(1 - (comp if landing else lax.div(index, 2)) + turn, 2)
         return pltpu.make_async_remote_copy(
-            src_ref=after.at[lax.rem(index, 2), wanted],
-            dst_ref=token.at[block, place, wanted],
-            send_sem=sent_out.at[block, turn, index],
-            recv_sem=came_out.at[block, turn, place],
+            src_ref=after.at[lax.rem(index, 2), wanted, lat],
+            dst_ref=token.at[block, place, wanted, lat],
+            send_sem=sent_out.at[block, turn, lat, index],
+            recv_sem=came_out.at[block, turn, lat, place],
             device_id=team_id(index),
             device_id_type=MESH,
         )
 
+    def band_peer(step):
+        x = lax.rem(me // 16 + step // 16, bands // 16)
+        y = lax.rem(lax.rem(me // 8, 2) + lax.rem(step // 8, 2), 2)
+        return x * 16 + y * 8 + lax.rem(lax.rem(me, 8) + lax.rem(step, 8), 8)
+
     def band_copy(source, target, sent, came, step, landing):
-        index = lax.rem(me + step, bands)
+        index = band_peer(step)
         return pltpu.make_async_remote_copy(
             src_ref=source.at[index],
             dst_ref=target.at[index if landing else me],
@@ -291,7 +296,7 @@
 
         def come(step, carry):
             band_copy(source, target, sent, came, step, True).wait()
-            widen(lax.rem(me + step, bands))
+            widen(band_peer(step))
             return carry
 
         lax.fori_loop(1, bands, come, 0)
@@ -318,7 +323,7 @@
     def tokens(block, lat):
         if block == 0:
             return turned_ref[lat]
-        pieces = [middle_in[s, lat].astype(jnp.float32) for s in range(4)]
+        pieces = [middle_in[lat, s].astype(jnp.float32) for s in range(4)]
         return jnp.concatenate(
             [jnp.concatenate([p[:quarter], doubled(p[quarter:])], axis=1) for p in pieces], axis=0
         )
@@ -425,9 +430,11 @@
                 tail = jnp.where(first_half, tail[:middle], swap(tail[middle:]))
                 after[s % 2, s // 2, lat, :quarter] = piece[:, :128].astype(jnp.bfloat16)
                 after[s % 2, s // 2, lat, quarter:] = tail.astype(jnp.bfloat16)
-        for turn in range(2):
             for step in range(1, 4):
-                out_copy(block, turn, step, False).start()
+                out_copy(block, 0, lat, step, False).start()
+        for lat in range(rows):
+            for step in range(1, 4):
+                out_copy(block, 1, lat, step, False).start()
         token[block, mine] = after[tile]
         for i in range(2):
             own_loads[2 * block + i].wait()
@@ -577,8 +584,9 @@
     )
 
     def halves(i, carry):
-        for step in range(1, 4):
-            out_copy(0, i, step, True).wait()
+        for lat in range(rows):
+            for step in range(1, 4):
+                out_copy(0, i, lat, step, True).wait()
         mlp(0, lax.rem(1 - comp + i, 2))
 
         @pl.when(i == 0)
@@ -688,6 +696,9 @@
             flat_ref[row] = field
             surface_ref[row] = field[:4]
 
+    def middle_args(lat):
+        return middle_out.at[lat], middle_in.at[lat], sent_middle.at[lat], came_middle.at[lat], "each"
+
     near = zeros((8, quarter))
     for lat in range(rows):
         both = jnp.concatenate([flat_ref[2 * lat], flat_ref[2 * lat + 1]], axis=0)
@@ -699,7 +710,9 @@
                 split_bf16(patch[e * quarter : (e + 1) * quarter]),
                 split_bf16(embed[e * 16 : (e + 1) * 16]),
             )
-        pack(total, lambda s, lat=lat: middle_out.at[s, lat])
+        pack(total, lambda s, lat=lat: middle_out.at[lat, s])
+        team_exchange(*middle_args(lat))
+        middle_in[lat, mine] = middle_out[lat, mine]
         rounded = total.astype(jnp.bfloat16)
         wide = rounded.astype(jnp.float32)
         high, low = split_bf16(wide * wide)
@@ -712,17 +725,16 @@
     near_args = (near_sums, all_near, sent_near, came_near, "whole")
     team_exchange(*near_args)
     all_near[mine] = near_sums[...]
-    args = (middle_out, middle_in, sent_middle, came_middle, "each")
-    team_exchange(*args)
-    middle_in[mine] = middle_out[mine]
-    team_finish(*args)
+    for lat in range(rows):
+        team_finish(*middle_args(lat))
     team_finish(*near_args)
 
     spectral_filter(1, lambda: None, lambda: None)
 
     def quarters(which_quarter, carry):
-        for step in range(1, 4):
-            out_copy(1, which_quarter, step, True).wait()
+        for lat in range(rows):
+            for step in range(1, 4):
+                out_copy(1, which_quarter, lat, step, True).wait()
         mlp(1, which_quarter)
         for lat in range(rows):
             pack(
@@ -817,8 +829,8 @@
         pltpu.VMEM((2, 2 * rows + 6, cells + 16, 128), single),
         pltpu.VMEM((2 * rows, cells, ocean_channels), single),
         pltpu.VMEM((2 * cells, waves), narrow),
-        pltpu.VMEM((4, rows, packed, 128), narrow),
-        pltpu.VMEM((4, rows, packed, 128), narrow),
+        pltpu.VMEM((rows, 4, packed, 128), narrow),
+        pltpu.VMEM((rows, 4, packed, 128), narrow),
         pltpu.VMEM((2, 8, channels), single),
         pltpu.VMEM((2, 8, 256), single),
         pltpu.VMEM((2, 2, 2 * slot, 2 * slot), narrow),
@@ -836,8 +848,8 @@
         pltpu.VMEM((cells + 16, 16), single),
         pltpu.VMEM((256, 128), single),
         dma(4), dma(4), dma(2, bands), dma(2, bands), dma(2, bands), dma(2, bands),
-        dma(2, 2, 4), dma(2, 2, 4), dma(1), dma(1), dma(2, 4), dma(2, 4), dma(2, 2), dma(2, 2), dma(2, 2),
-        dma(4), dma(4), dma(8), dma(8), dma(8), dma(8), dma(8), dma(8), dma(4), dma(4),
+        dma(2, 2, rows, 4), dma(2, 2, rows, 4), dma(1), dma(1), dma(2, 4), dma(2, 4), dma(2, 2), dma(2, 2), dma(2, 2),
+        dma(4), dma(4), dma(8), dma(8), dma(8), dma(8), dma(8), dma(8), dma(rows, 4), dma(rows, 4),
         dma(4), dma(4),
     ]
     atmosphere_next, ocean_next, surface = pl.pallas_call(

time: 178 us -> 182 us (1.022)
  Pallas kernels: 170 us -> 175 us
    pallas_call x1, Pallas kernels: 170 us -> 175 us  [on_device(): pl.pallas_call(functools.partial(step_kernel, bands), out_shape=(jax.Shap...]
where the time goes in v5:
time: 182 us; the launch traced here: 181 us
  Pallas kernels  175 us (96%)
  local copies, waits for them, and re-layouts  5.32 us (3%)
    pallas_call x1, Pallas kernels, on_device(): pl.pallas_call(functools.partial(step_kernel, bands), out_shape=(jax.Shap...  175 us
    unnamed x3, local copies, waits for them, and re-layouts  5.32 us

profile of v5, /device:TPU:1, one launch (start us, length us, event | category | flops | bytes accessed | tf_op | source)
XLA Modules:
  0.0 181.5 jit_solution(4221984569849194286)
XLA Ops:
  0.6 175.5 %shard_map.265 = (bf16[3,384,192]{2,1,0:T(8,128)(2,1)}, bf16[6,192,256]{2,1,0:T(8,128)(2,1)}, f32[6,4,192]{2,1,0:T(4,128)}) custom-call(bf16[3,192,384]{2,1,0:T(8,128)(2,1)} %bitcast.7, f32[2,2,2,192,96]{4,3,2,1,0:T(8,128)} %refs_1_.1, f32[2,2,2,192]{3,2,1,0:T(2,128)} %refs_2_.1, f32[2,2,768]{2,1,0:T(2,128)} %refs_3_.1, f32[2,2,768]{2,1,0:T(2,128)} %refs_4_.1, ...), custom_call_target="tpu_custom_call" | custom-call | tf_op jit(solution)/shard_map/pallas_call | solution.py:855
  176.1 2.1 %copy.29 = bf16[3,384,192]{1,2,0:T(8,128)(2,1)} copy(bf16[3,384,192]{2,1,0:T(8,128)(2,1)} %get-tuple-element.9) | data formatting | bytes 884736
  178.2 1.9 %copy.32 = bf16[6,192,256]{2,1,0:T(8,128)(2,1)} copy(bf16[6,192,256]{2,1,0:T(8,128)(2,1)} %get-tuple-element.16) | data formatting | bytes 1179648
  180.1 1.3 copy.33

commit v6 on v4

--- a/solution.py
+++ b/solution.py
@@ -261,8 +261,15 @@
             device_id_type=MESH,
         )
 
+    my_x, my_y, my_z = lax.div(me, 16), lax.rem(lax.div(me, 8), 2), lax.rem(me, 8)
+
+    def band_peer(step):
+        x = lax.rem(my_x + lax.div(step, 16), bands // 16)
+        y = lax.rem(my_y + lax.div(step, 8), 2)
+        return x * 16 + y * 8 + lax.rem(my_z + step, 8)
+
     def band_copy(source, target, sent, came, step, landing):
-        index = lax.rem(me + step, bands)
+        index = band_peer(step)
         return pltpu.make_async_remote_copy(
             src_ref=source.at[index],
             dst_ref=target.at[index if landing else me],
@@ -291,7 +298,7 @@
 
         def come(step, carry):
             band_copy(source, target, sent, came, step, True).wait()
-            widen(lax.rem(me + step, bands))
+            widen(band_peer(step))
             return carry
 
         lax.fori_loop(1, bands, come, 0)

time: 178 us -> 179 us (level)
  Pallas kernels: 170 us -> 172 us
    pallas_call x1, Pallas kernels: 170 us -> 172 us  [on_device(): pl.pallas_call(functools.partial(step_kernel, bands), out_shape=(jax.Shap...]
where the time goes in v6:
time: 179 us; the launch traced here: 178 us
  Pallas kernels  172 us (96%)
  local copies, waits for them, and re-layouts  5.32 us (3%)
    pallas_call x1, Pallas kernels, on_device(): pl.pallas_call(functools.partial(step_kernel, bands), out_shape=(jax.Shap...  172 us
    unnamed x3, local copies, waits for them, and re-layouts  5.32 us

profile of v6, /device:TPU:1, one launch (start us, length us, event | category | flops | bytes accessed | tf_op | source)
XLA Modules:
  0.0 178.2 jit_solution(14605889446884059523)
XLA Ops:
  0.6 172.3 %shard_map.265 = (bf16[3,384,192]{2,1,0:T(8,128)(2,1)}, bf16[6,192,256]{2,1,0:T(8,128)(2,1)}, f32[6,4,192]{2,1,0:T(4,128)}) custom-call(bf16[3,192,384]{2,1,0:T(8,128)(2,1)} %bitcast.7, f32[2,2,2,192,96]{4,3,2,1,0:T(8,128)} %refs_1_.1, f32[2,2,2,192]{3,2,1,0:T(2,128)} %refs_2_.1, f32[2,2,768]{2,1,0:T(2,128)} %refs_3_.1, f32[2,2,768]{2,1,0:T(2,128)} %refs_4_.1, ...), custom_call_target="tpu_custom_call" | custom-call | tf_op jit(solution)/shard_map/pallas_call | solution.py:850
  172.9 2.1 %copy.29 = bf16[3,384,192]{1,2,0:T(8,128)(2,1)} copy(bf16[3,384,192]{2,1,0:T(8,128)(2,1)} %get-tuple-element.9) | data formatting | bytes 884736
  175.0 1.9 %copy.32 = bf16[6,192,256]{2,1,0:T(8,128)(2,1)} copy(bf16[6,192,256]{2,1,0:T(8,128)(2,1)} %get-tuple-element.16) | data formatting | bytes 1179648
  176.9 1.3 copy.33
